TPU v7x, 256 devices: a whole 4x4x8 slice. The times are simulated.
256 devices in a mesh: tile: 64 (over y, z, core), cuts: 4 (over x).
Axes of the slice: x: 4, y: 4, z: 8, core: 2. Of those that a mesh axis runs over, the one named last changes fastest.
Arguments:
- object_slices: float32 [8, 2, 16384, 256], P('cuts', None, 'tile'), may hold values from -1 to 1, as said below
- probe_field: float32 [2, 256, 256], replicated, may hold values from -6 to 6
- row_offsets: int32 [256], P('tile'), may hold values from 0 to 255, as said below
- columns: int32 [256], P('tile'), may hold values from 0 to 0
- counts: int32 [64], P('tile'), may hold values from 1 to 4, 128 in all
- amplitudes: bfloat16 [256, 256, 256], P('tile'), may hold values from 0.25 to 4
Outputs:
- new_object: float32 [8, 2, 16384, 256], P('cuts', None, 'tile')
Inputs may be any that keep to these rules, and one draw needn't show every extreme that they name: `row_offsets`: the patch of slot k of block b starts at object row b * 256 + value; in the last block values are at most 0, so every patch lies inside the object and inside its own tile and the next one. `counts`: block b uses its first value slots; the others are padding. The values sum to 128. `object_slices`: every entry has magnitude at most 1.
All inputs are finite; a program needn't handle non-finite values.
Results may differ from a plain program's by a relative error of at most 0.015.
Values may be sent and summed in bfloat16 or wider, within the bound.
No kernel may reach another device: no remote copies, remote signals or barrier semaphores. Data moves between devices by JAX's collectives and lax.ppermute only.
A program may use at most 64 MiB of HBM per device.

v0:
```python
from functools import partial
import math

import jax
import jax.numpy as jnp
import numpy as np
from jax import lax
from jax.experimental import pallas as pl
from jax.experimental.pallas import tpu as pltpu
from jax.sharding import PartitionSpec as P


PAT = 256
ITERS = 2
CUTS = 4
LOCAL = 2
SMALL = 4
LARGE = 12
SLICES = CUTS * LOCAL

object_rate = 0.25


f32 = jnp.float32
bf16 = jnp.bfloat16
VMEM = pltpu.MemorySpace.VMEM
SMEM = pltpu.MemorySpace.SMEM


def tables(size):
    index = np.arange(size)
    angle = (index[:, None] * index[None, :] % size) * (2.0 * math.pi / size)
    cosine, sine = np.cos(angle), np.sin(angle)
    signed = np.where(index < size // 2, index, index - size)
    phase = (signed * signed % (8 * size)) * (-math.pi / (4.0 * size))
    filter_re, filter_im = np.cos(phase), np.sin(phase)
    kernel_re = (filter_re @ cosine - filter_im @ sine) / size
    kernel_im = (filter_re @ sine + filter_im @ cosine) / size
    offset = (index[:, None] - index[None, :]) % size
    norm = 1.0 / math.sqrt(size)
    four = np.stack([cosine * norm, -sine * norm])
    kern = np.stack([kernel_re[offset], kernel_im[offset]])
    return np.stack([four, kern]).astype(np.float32).astype(bf16)


def shift(block, axis, distance):
    size = lax.axis_size(axis)
    return lax.ppermute(block, axis, [(i, (i + distance) % size) for i in range(size)])


def step(block, axis, distance):
    devices = range(lax.axis_size(axis))
    route = [(i - distance, i) for i in devices if i - distance in devices]
    return lax.ppermute(block, axis, route)


def chunks(size):
    for m in range(0, PAT, size):
        yield pl.ds(m, size), m + lax.broadcasted_iota(jnp.int32, (size, PAT), 0)


def cut_windows(own, margin, rows, place, offsets_ref, outs, j):
    for d in range(CUTS):
        outs[d][j, place] = jnp.where(rows >= offsets_ref[d], own, margin).astype(bf16)


def pack_kernel(i, offsets_ref, own_ref, margin_ref, *outs):
    for j in range(2):
        for place, rows in chunks(32):
            own = own_ref[i, j, place]
            cut_windows(own, margin_ref[j, place].astype(f32), rows, place, offsets_ref, outs, j)


def update_part(i, offsets_ref, own_ref, margin_ref, sum_ref, spill_ref, spill_in_ref, sum_in_ref,
                new_ref, *outs):
    for j in range(2):
        for place, rows in chunks(32):
            arrived = sum_ref[j, place] + spill_in_ref[j, place].astype(f32)
            own = own_ref[i, j, place] - object_rate * arrived
            new_ref[j, place] = own
            beyond = sum_in_ref[j, place].astype(f32) + spill_ref[j, place].astype(f32)
            margin = margin_ref[j, place].astype(f32) - object_rate * beyond
            cut_windows(own, margin, rows, place, offsets_ref, outs, j)


def sum_part(offsets_ref, *rest):
    parts, sum_ref, sum16_ref, spill_ref = rest[:CUTS], *rest[CUTS:]
    for j in range(2):
        for place, rows in chunks(32):
            own, spill = 0.0, 0.0
            for d in range(CUTS):
                part = parts[d][j, place].astype(f32)
                here = rows >= offsets_ref[d]
                own = own + jnp.where(here, part, 0.0)
                spill = spill + jnp.where(here, 0.0, part)
            sum_ref[j, place] = own
            sum16_ref[j, place] = own.astype(bf16)
            spill_ref[j, place] = spill.astype(bf16)


def middle_kernel(ahead_ref, behind_ref, *rest):
    ins, outs = rest[: 6 + CUTS], rest[6 + CUTS :]
    update_part(0, ahead_ref, *ins[:6], *outs[: 1 + CUTS])
    sum_part(behind_ref, *ins[6:], *outs[1 + CUTS :])


def finish_kernel(*rest):
    new_ref = rest[-1]
    for i in range(LOCAL):
        own_ref, sum_ref, spill_in_ref = rest[3 * i : 3 * i + 3]
        arrived = sum_ref[...] + spill_in_ref[...].astype(f32)
        new_ref[i] = own_ref[...] - object_rate * arrived


def prepare_kernel(scalars_ref, tables_ref, probe_ref, mats_ref, start_ref):
    turn = scalars_ref[2]

    def put(m, re, im):
        mats_ref[m, :PAT, :PAT] = re
        mats_ref[m, :PAT, PAT:] = -im
        mats_ref[m, PAT:, :PAT] = im
        mats_ref[m, PAT:, PAT:] = re

    four_re, four_im = tables_ref[0, 0], tables_ref[0, 1]
    wide_re, wide_im = four_re.astype(f32), four_im.astype(f32)
    put(0, pltpu.roll(wide_re, turn, 1).astype(bf16), pltpu.roll(wide_im, turn, 1).astype(bf16))
    put(1, four_re, -four_im)
    put(2, pltpu.roll(wide_re, turn, 0).astype(bf16), -pltpu.roll(wide_im, turn, 0).astype(bf16))
    put(3, four_re, four_im)
    put(4, tables_ref[1, 0], tables_ref[1, 1])
    put(5, tables_ref[1, 0], -tables_ref[1, 1])
    for j in range(2):
        start_ref[j * PAT : (j + 1) * PAT] = pltpu.roll(probe_ref[j], turn, 0).astype(bf16)


CHUNK = 32


def transform(left, right, field, inner):
    for half in (slice(0, PAT), slice(PAT, 2 * PAT)):
        mid = jnp.dot(left[half], field[...], preferred_element_type=f32)
        inner[:, half] = mid.astype(bf16)
    return [
        jnp.dot(inner[...], right[:, half], preferred_element_type=f32)
        for half in (slice(0, PAT), slice(PAT, 2 * PAT))
    ]


def slot_kernel(scalars_ref, mats, start_ref, amplitudes_ref, *rest):
    count = CUTS * LOCAL
    sources, results = rest[:count], rest[count : 2 * count]
    window, saved, terms, field, inner, amplitude, in_sem, out_sem, side_sem = rest[2 * count :]
    cut = scalars_ref[0]
    live = scalars_ref[1]

    @pl.when(live == 0)
    def _():
        terms[0, 0] = jnp.zeros(PLANE, bf16)
        copies = [
            pltpu.make_async_copy(terms.at[0, 0], results[n], out_sem.at[n]) for n in range(count)
        ]
        for copy in copies:
            copy.start()
        for copy in copies:
            copy.wait()

    @pl.when(live != 0)
    def _():
        side = pltpu.make_async_copy(amplitudes_ref.at[cut], amplitude, side_sem)
        for n in range(count):
            i, d = n // CUTS, n % CUTS
            owner = lax.rem(cut - d + CUTS, CUTS)
            pltpu.make_async_copy(
                sources[n], window.at[owner, i], in_sem.at[owner * LOCAL + i]
            ).start()
        side.start()
        four_in, four_in_right, four_out, four_out_right, kern, kern_conj = (
            mats.at[m] for m in range(6)
        )

        def arrive(s):
            pltpu.make_async_copy(sources[0], window.at[s // LOCAL, s % LOCAL], in_sem.at[s]).wait()

        def leave(s):
            turn = lax.rem(s // LOCAL - cut + CUTS, CUTS)
            for n in range(count):
                i, d = n // CUTS, n % CUTS

                @pl.when((turn == d) & (s % LOCAL == i))
                def _():
                    pltpu.make_async_copy(
                        terms.at[s // LOCAL, s % LOCAL], results[n], out_sem.at[n]
                    ).start()

        def piece(s, m):
            rows = pl.ds(m, CHUNK)
            place = (s // LOCAL, s % LOCAL)
            return window[place + (0, rows)].astype(f32), window[place + (1, rows)].astype(f32)

        def put(m, re, im):
            field[m : m + CHUNK] = re.astype(bf16)
            field[PAT + m : PAT + m + CHUNK] = im.astype(bf16)

        def multiply(s, m, re, im):
            w_re, w_im = piece(s, m)
            put(m, re * w_re - im * w_im, re * w_im + im * w_re)

        def parts(out):
            for m in range(0, PAT, CHUNK):
                yield m, out[0][m : m + CHUNK], out[1][m : m + CHUNK]

        def gather(s, out):
            for m, g_re, g_im in parts(out):
                re = saved[s, m : m + CHUNK].astype(f32)
                im = saved[s, PAT + m : PAT + m + CHUNK].astype(f32)
                place = (s // LOCAL, s % LOCAL)
                rows = pl.ds(m, CHUNK)
                terms[place + (0, rows)] = (re * g_re + im * g_im).astype(bf16)
                terms[place + (1, rows)] = (re * g_im - im * g_re).astype(bf16)
                w_re, w_im = piece(s, m)
                put(m, w_re * g_re + w_im * g_im, w_re * g_im - w_im * g_re)

        saved[0] = start_ref[...]
        arrive(0)
        for m in range(0, PAT, CHUNK):
            re = start_ref[m : m + CHUNK].astype(f32)
            im = start_ref[PAT + m : PAT + m + CHUNK].astype(f32)
            multiply(0, m, re, im)

        def forward(s, carry):
            arrive(s)
            out = transform(kern, kern_conj, field, inner)
            for m, re, im in parts(out):
                saved[s, m : m + CHUNK] = re.astype(bf16)
                saved[s, PAT + m : PAT + m + CHUNK] = im.astype(bf16)
                multiply(s, m, re, im)
            return carry

        lax.fori_loop(1, SLICES, forward, 0)
        side.wait()
        far = transform(four_in, four_in_right, field, inner)
        for m, re, im in parts(far):
            scale = lax.rsqrt(re * re + im * im + 1.0)
            factor = 1.0 - amplitude[m : m + CHUNK].astype(f32) * scale
            put(m, re * factor, im * factor)
        gather(SLICES - 1, transform(four_out, four_out_right, field, inner))
        leave(SLICES - 1)

        def backward(i, carry):
            gather(SLICES - 1 - i, transform(kern_conj, kern, field, inner))
            leave(SLICES - 1 - i)
            return carry

        lax.fori_loop(1, SLICES, backward, 0)
        for n in range(count):
            pltpu.make_async_copy(terms.at[0, 0], results[n], out_sem.at[n]).wait()


PLANE = (2, PAT, PAT)
BLOCK = (LOCAL,) + PLANE
plane16 = jax.ShapeDtypeStruct(PLANE, bf16)
plane32 = jax.ShapeDtypeStruct(PLANE, f32)
block32 = jax.ShapeDtypeStruct(BLOCK, f32)


def limit(mib):
    return pltpu.CompilerParams(vmem_limit_bytes=mib * 1024 * 1024)


def vmem(count):
    return [pl.BlockSpec(memory_space=VMEM)] * count


def smem(count=1):
    return [pl.BlockSpec(memory_space=SMEM)] * count


def anywhere(count):
    return [pl.BlockSpec(memory_space=pl.ANY)] * count


def in_hbm(array):
    return pltpu.with_memory_space_constraint(array, pltpu.MemorySpace.HBM)


def pack(i, offsets, own, margin):
    return pl.pallas_call(
        partial(pack_kernel, i),
        compiler_params=limit(SMALL),
        out_shape=[plane16] * CUTS,
        in_specs=smem() + vmem(2),
        out_specs=vmem(CUTS),
    )(offsets, own, margin)


def update(i, offsets, *arrays):
    return pl.pallas_call(
        partial(update_part, i),
        compiler_params=limit(SMALL),
        out_shape=[plane32] + [plane16] * CUTS,
        in_specs=smem() + vmem(6),
        out_specs=vmem(1 + CUTS),
    )(offsets, *arrays)


def add_up(offsets, parts):
    return pl.pallas_call(
        sum_part,
        compiler_params=limit(SMALL),
        out_shape=[plane32, plane16, plane16],
        in_specs=smem() + vmem(CUTS),
        out_specs=vmem(3),
    )(offsets, *parts)


def middle(ahead, behind, *arrays):
    return pl.pallas_call(
        middle_kernel,
        compiler_params=limit(SMALL),
        out_shape=[plane32] + [plane16] * CUTS + [plane32, plane16, plane16],
        in_specs=smem(2) + vmem(6 + CUTS),
        out_specs=vmem(4 + CUTS),
    )(ahead, behind, *arrays)


def finish(*arrays):
    return pl.pallas_call(
        finish_kernel, compiler_params=limit(SMALL), out_shape=block32, in_specs=vmem(3 * LOCAL), out_specs=vmem(1)[0]
    )(*arrays)


def prepare(scalars, tabs, probe):
    return pl.pallas_call(
        prepare_kernel,
        compiler_params=limit(SMALL),
        out_shape=[
            jax.ShapeDtypeStruct((6, 2 * PAT, 2 * PAT), bf16),
            jax.ShapeDtypeStruct((2 * PAT, PAT), bf16),
        ],
        in_specs=smem() + vmem(2),
        out_specs=vmem(2),
    )(scalars, tabs, probe)


def run_slot(scalars, mats, start, amplitudes, windows):
    count = CUTS * LOCAL
    return pl.pallas_call(
        slot_kernel,
        compiler_params=limit(LARGE),
        out_shape=[plane16] * count,
        in_specs=smem()
        + vmem(2)
        + anywhere(1 + count),
        out_specs=anywhere(count),
        scratch_shapes=[
            pltpu.VMEM((CUTS,) + BLOCK, bf16),
            pltpu.VMEM((SLICES, 2 * PAT, PAT), bf16),
            pltpu.VMEM((CUTS,) + BLOCK, bf16),
            pltpu.VMEM((2 * PAT, PAT), bf16),
            pltpu.VMEM((PAT, 2 * PAT), bf16),
            pltpu.VMEM((PAT, PAT), bf16),
            pltpu.SemaphoreType.DMA((count,)),
            pltpu.SemaphoreType.DMA((count,)),
            pltpu.SemaphoreType.DMA,
        ],
    )(scalars, mats, start, in_hbm(amplitudes), *windows)


def exchange(blocks):
    arrived = [blocks[0]]
    for d in range(1, CUTS):
        arrived.append(shift(blocks[d], "cuts", d))
    return arrived


def run(object_slices, probe_field, row_offsets, columns, counts, amplitudes):
    tabs = jnp.asarray(tables(PAT))
    cut = lax.axis_index("cuts").astype(jnp.int32)
    turn = jnp.arange(CUTS, dtype=jnp.int32)
    ahead = row_offsets[(cut + turn) % CUTS]
    behind = row_offsets[(cut - turn + CUTS) % CUTS]
    live = (cut < counts[0]).astype(jnp.int32)
    scalars = jnp.stack([cut, live, ahead[0]])
    constants = prepare(scalars, tabs, probe_field)
    each = range(LOCAL)
    margins = [step(object_slices[i].astype(bf16), "tile", -1) for i in each]
    windows = []
    for i in each:
        windows += exchange(pack(i, ahead, object_slices, margins[i]))
    for iteration in range(ITERS):
        terms = run_slot(scalars, *constants, amplitudes, windows)
        first, second = (exchange(terms[CUTS * i : CUTS * (i + 1)]) for i in each)
        total_a, total16_a, spill_a = add_up(behind, first)
        spill_in_a = step(spill_a, "tile", 1)
        if iteration + 1 < ITERS:
            total_in_a = step(total16_a, "tile", -1)
            out = middle(
                ahead, behind, object_slices, margins[0], total_a, spill_a, spill_in_a,
                total_in_a, *second
            )
            own_a, cut_a, (total_b, total16_b, spill_b) = out[0], out[1 : 1 + CUTS], out[1 + CUTS :]
            spill_in_b = step(spill_b, "tile", 1)
            total_in_b = step(total16_b, "tile", -1)
            windows = exchange(cut_a)
            own_b, *cut_b = update(
                1, ahead, object_slices, margins[1], total_b, spill_b, spill_in_b, total_in_b
            )
            windows += exchange(cut_b)
            again, own_a = lax.optimization_barrier((scalars, own_a))
            constants = prepare(again, tabs, probe_field)
    total_b, _, spill_b = add_up(behind, second)
    spill_in_b = step(spill_b, "tile", 1)
    return finish(own_a, total_a, spill_in_a, own_b, total_b, spill_in_b)


def solution(mesh):
    in_specs = (
        P("cuts", None, "tile", None),
        P(),
        P("tile"),
        P("tile"),
        P("tile"),
        P("tile", None, None),
    )
    out_specs = P("cuts", None, "tile", None)
    return jax.shard_map(run, mesh=mesh, in_specs=in_specs, out_specs=out_specs, check_vma=False)
```

profile of v0, /device:TPU:18, one launch (start us, length us, event | category | flops | bytes accessed | tf_op | source)
XLA Modules:
  0.0 170.8 jit_solution(13087795114681527430)
XLA Ops:
  2.2 7.1 %collective-permute-start = (bf16[2,256,256]{2,1,0:T(8,128)(2,1)S(1)}, bf16[2,256,256]{2,1,0:T(8,128)(2,1)S(1)}, u32[]{:S(2)}, u32[]{:S(2)}) collective-permute-start(bf16[2,256,256]{2,1,0:T(8,128)(2,1)S(1)} %get-tuple-element.106), channel_id=1, source_target_pairs={{4,0},{8,4},{12,8},{16,12},{20,16},{24,20},{28,24},{32,28},{36,32}... | collective-permute-start | bytes 786440 | tf_op jit(solution)/shard_map/ppermute | solution.py:54
  9.3 2.6 %collective-permute-start.4 = (bf16[2,256,256]{2,1,0:T(8,128)(2,1)}, bf16[2,256,256]{2,1,0:T(8,128)(2,1)S(1)}, u32[]{:S(2)}, u32[]{:S(2)}) collective-permute-start(bf16[2,256,256]{2,1,0:T(8,128)(2,1)} %get-tuple-element.105), channel_id=1, source_target_pairs={{4,0},{8,4},{12,8},{16,12},{20,16},{24,20},{28,24},{32,28},{36,32}... | collective-permute-start | bytes 786440 | tf_op jit(solution)/shard_map/ppermute | solution.py:54
  17.2 2.2 %collective-permute-start.3 = (bf16[2,256,256]{2,1,0:T(8,128)(2,1)}, bf16[2,256,256]{2,1,0:T(8,128)(2,1)}, u32[]{:S(2)}, u32[]{:S(2)}) collective-permute-start(bf16[2,256,256]{2,1,0:T(8,128)(2,1)} %get-tuple-element.60), channel_id=1, source_target_pairs={{0,3},{1,0},{2,1},{3,2},{4,7},{5,4},{6,5},{7,6},{8,11},{9,8},{10,9... | collective-permute-start | bytes 786440 | tf_op jit(solution)/shard_map/ppermute | solution.py:48
  21.6 3.5 %collective-permute-start.6 = (bf16[2,256,256]{2,1,0:T(8,128)(2,1)}, bf16[2,256,256]{2,1,0:T(8,128)(2,1)}, u32[]{:S(2)}, u32[]{:S(2)}) collective-permute-start(bf16[2,256,256]{2,1,0:T(8,128)(2,1)} %get-tuple-element.63), channel_id=1, source_target_pairs={{0,2},{1,3},{2,0},{3,1},{4,6},{5,7},{6,4},{7,5},{8,10},{9,11},{10,... | collective-permute-start | bytes 786440 | tf_op jit(solution)/shard_map/ppermute | solution.py:48
  28.6 4.2 %collective-permute-done.3.rest_3_ = bf16[2,256,256]{2,1,0:T(8,128)(2,1)} collective-permute-done((bf16[2,256,256]{2,1,0:T(8,128)(2,1)}, bf16[2,256,256]{2,1,0:T(8,128)(2,1)}, u32[]{:S(2)}, u32[]{:S(2)}) %collective-permute-start.3) | collective-permute-done | bytes 262176 | tf_op jit(solution)/shard_map/ppermute | solution.py:48
  32.8 2.4 %collective-permute-done.5.rest_5_ = bf16[2,256,256]{2,1,0:T(8,128)(2,1)} collective-permute-done((bf16[2,256,256]{2,1,0:T(8,128)(2,1)}, bf16[2,256,256]{2,1,0:T(8,128)(2,1)}, u32[]{:S(2)}, u32[]{:S(2)}) %collective-permute-start.5) | collective-permute-done | bytes 262176 | tf_op jit(solution)/shard_map/ppermute | solution.py:48
  35.2 3.2 %collective-permute-done.6.rest_6_ = bf16[2,256,256]{2,1,0:T(8,128)(2,1)} collective-permute-done((bf16[2,256,256]{2,1,0:T(8,128)(2,1)}, bf16[2,256,256]{2,1,0:T(8,128)(2,1)}, u32[]{:S(2)}, u32[]{:S(2)}) %collective-permute-start.6) | collective-permute-done | bytes 262176 | tf_op jit(solution)/shard_map/ppermute | solution.py:48
  38.4 2.9 %collective-permute-done.7.rest_7_ = bf16[2,256,256]{2,1,0:T(8,128)(2,1)} collective-permute-done((bf16[2,256,256]{2,1,0:T(8,128)(2,1)}, bf16[2,256,256]{2,1,0:T(8,128)(2,1)}, u32[]{:S(2)}, u32[]{:S(2)}) %collective-permute-start.7) | collective-permute-done | bytes 262176 | tf_op jit(solution)/shard_map/ppermute | solution.py:48
  48.6 10.0 %collective-permute-start.9 = (bf16[2,256,256]{2,1,0:T(8,128)(2,1)}, bf16[2,256,256]{2,1,0:T(8,128)(2,1)S(1)}, u32[]{:S(2)}, u32[]{:S(2)}) collective-permute-start(bf16[2,256,256]{2,1,0:T(8,128)(2,1)} %get-tuple-element.67), channel_id=1, source_target_pairs={{0,2},{1,3},{2,0},{3,1},{4,6},{5,7},{6,4},{7,5},{8,10},{9,11},{10,... | collective-permute-start | bytes 786440 | tf_op jit(solution)/shard_map/ppermute | solution.py:48
  59.3 2.0 %collective-permute-start.13 = (bf16[2,256,256]{2,1,0:T(8,128)(2,1)}, bf16[2,256,256]{2,1,0:T(8,128)(2,1)S(1)}, u32[]{:S(2)}, u32[]{:S(2)}) collective-permute-start(bf16[2,256,256]{2,1,0:T(8,128)(2,1)} %copy-done.12), channel_id=1, source_target_pairs={{0,1},{1,2},{2,3},{3,0},{4,5},{5,6},{6,7},{7,4},{8,9},{9,10},{10,1... | collective-permute-start | bytes 786440 | tf_op jit(solution)/shard_map/ppermute | solution.py:48
  62.8 9.5 %collective-permute-start.15 = (bf16[2,256,256]{2,1,0:T(8,128)(2,1)}, bf16[2,256,256]{2,1,0:T(8,128)(2,1)S(1)}, u32[]{:S(2)}, u32[]{:S(2)}) collective-permute-start(bf16[2,256,256]{2,1,0:T(8,128)(2,1)} %copy-done.10), channel_id=1, source_target_pairs={{0,3},{1,0},{2,1},{3,2},{4,7},{5,4},{6,5},{7,6},{8,11},{9,8},{10,9... | collective-permute-start | bytes 786440 | tf_op jit(solution)/shard_map/ppermute | solution.py:48
  74.3 4.5 %collective-permute-start.12 = (bf16[2,256,256]{2,1,0:T(8,128)(2,1)S(1)}, bf16[2,256,256]{2,1,0:T(8,128)(2,1)S(1)}, u32[]{:S(2)}, u32[]{:S(2)}) collective-permute-start(bf16[2,256,256]{2,1,0:T(8,128)(2,1)S(1)} %get-tuple-element.71), channel_id=1, source_target_pairs={{4,0},{8,4},{12,8},{16,12},{20,16},{24,20},{28,24},{32,28},{36,32}... | collective-permute-start | bytes 786440 | tf_op jit(solution)/shard_map/ppermute | solution.py:54
  78.8 1.9 %collective-permute-start.11 = (bf16[2,256,256]{2,1,0:T(8,128)(2,1)S(1)}, bf16[2,256,256]{2,1,0:T(8,128)(2,1)S(1)}, u32[]{:S(2)}, u32[]{:S(2)}) collective-permute-start(bf16[2,256,256]{2,1,0:T(8,128)(2,1)S(1)} %get-tuple-element.70.rest_3_), channel_id=1, source_target_pairs={{0,4},{4,8},{8,12},{12,16},{16,20},{20,24},{24,28},{28,32},{32,36}... | collective-permute-start | bytes 786440 | tf_op jit(solution)/shard_map/ppermute | solution.py:54
  80.8 2.1 %collective-permute-done.15.rest_9_ = bf16[2,256,256]{2,1,0:T(8,128)(2,1)S(1)} collective-permute-done((bf16[2,256,256]{2,1,0:T(8,128)(2,1)}, bf16[2,256,256]{2,1,0:T(8,128)(2,1)S(1)}, u32[]{:S(2)}, u32[]{:S(2)}) %collective-permute-start.15) | collective-permute-done | bytes 262176 | tf_op jit(solution)/shard_map/ppermute | solution.py:48
  82.9 5.7 %collective-permute-done.11.rest_4_ = bf16[2,256,256]{2,1,0:T(8,128)(2,1)S(1)} collective-permute-done((bf16[2,256,256]{2,1,0:T(8,128)(2,1)S(1)}, bf16[2,256,256]{2,1,0:T(8,128)(2,1)S(1)}, u32[]{:S(2)}, u32[]{:S(2)}) %collective-permute-start.11) | collective-permute-done | bytes 262176 | tf_op jit(solution)/shard_map/ppermute | solution.py:54
  90.8 1.9 %collective-permute-start.20 = (bf16[2,256,256]{2,1,0:T(8,128)(2,1)S(1)}, bf16[2,256,256]{2,1,0:T(8,128)(2,1)S(1)}, u32[]{:S(2)}, u32[]{:S(2)}) collective-permute-start(bf16[2,256,256]{2,1,0:T(8,128)(2,1)S(1)} %get-tuple-element.87), channel_id=1, source_target_pairs={{4,0},{8,4},{12,8},{16,12},{20,16},{24,20},{28,24},{32,28},{36,32}... | collective-permute-start | bytes 786440 | tf_op jit(solution)/shard_map/ppermute | solution.py:54
  92.8 2.4 %collective-permute-start.19 = (bf16[2,256,256]{2,1,0:T(8,128)(2,1)S(1)}, bf16[2,256,256]{2,1,0:T(8,128)(2,1)S(1)}, u32[]{:S(2)}, u32[]{:S(2)}) collective-permute-start(bf16[2,256,256]{2,1,0:T(8,128)(2,1)S(1)} %get-tuple-element.86.spill_ref), channel_id=1, source_target_pairs={{0,4},{4,8},{8,12},{12,16},{16,20},{20,24},{24,28},{28,32},{32,36}... | collective-permute-start | bytes 786440 | tf_op jit(solution)/shard_map/ppermute | solution.py:54
  97.1 2.0 %collective-permute-start.18 = (bf16[2,256,256]{2,1,0:T(8,128)(2,1)S(1)}, bf16[2,256,256]{2,1,0:T(8,128)(2,1)S(1)}, u32[]{:S(2)}, u32[]{:S(2)}) collective-permute-start(bf16[2,256,256]{2,1,0:T(8,128)(2,1)S(1)} %get-tuple-element.84), channel_id=1, source_target_pairs={{0,3},{1,0},{2,1},{3,2},{4,7},{5,4},{6,5},{7,6},{8,11},{9,8},{10,9... | collective-permute-start | bytes 786440 | tf_op jit(solution)/shard_map/ppermute | solution.py:48
  99.1 3.5 %collective-permute-done.19.spill_in_ref = bf16[2,256,256]{2,1,0:T(8,128)(2,1)S(1)} collective-permute-done((bf16[2,256,256]{2,1,0:T(8,128)(2,1)S(1)}, bf16[2,256,256]{2,1,0:T(8,128)(2,1)S(1)}, u32[]{:S(2)}, u32[]{:S(2)}) %collective-permute-start.19) | collective-permute-done | bytes 262176 | tf_op jit(solution)/shard_map/ppermute | solution.py:54
  105.3 2.0 %collective-permute-start.23 = (bf16[2,256,256]{2,1,0:T(8,128)(2,1)S(1)}, bf16[2,256,256]{2,1,0:T(8,128)(2,1)S(1)}, u32[]{:S(2)}, u32[]{:S(2)}) collective-permute-start(bf16[2,256,256]{2,1,0:T(8,128)(2,1)S(1)} %get-tuple-element.91), channel_id=1, source_target_pairs={{0,3},{1,0},{2,1},{3,2},{4,7},{5,4},{6,5},{7,6},{8,11},{9,8},{10,9... | collective-permute-start | bytes 786440 | tf_op jit(solution)/shard_map/ppermute | solution.py:48
  108.4 3.9 %collective-permute-done.18.rest_3_ = bf16[2,256,256]{2,1,0:T(8,128)(2,1)S(1)} collective-permute-done((bf16[2,256,256]{2,1,0:T(8,128)(2,1)S(1)}, bf16[2,256,256]{2,1,0:T(8,128)(2,1)S(1)}, u32[]{:S(2)}, u32[]{:S(2)}) %collective-permute-start.18) | collective-permute-done | bytes 262176 | tf_op jit(solution)/shard_map/ppermute | solution.py:48
  112.3 3.4 %collective-permute-done.21.rest_5_ = bf16[2,256,256]{2,1,0:T(8,128)(2,1)S(1)} collective-permute-done((bf16[2,256,256]{2,1,0:T(8,128)(2,1)S(1)}, bf16[2,256,256]{2,1,0:T(8,128)(2,1)S(1)}, u32[]{:S(2)}, u32[]{:S(2)}) %collective-permute-start.21) | collective-permute-done | bytes 262176 | tf_op jit(solution)/shard_map/ppermute | solution.py:48
  115.7 2.2 %collective-permute-done.22.rest_6_ = bf16[2,256,256]{2,1,0:T(8,128)(2,1)S(1)} collective-permute-done((bf16[2,256,256]{2,1,0:T(8,128)(2,1)S(1)}, bf16[2,256,256]{2,1,0:T(8,128)(2,1)S(1)}, u32[]{:S(2)}, u32[]{:S(2)}) %collective-permute-start.22) | collective-permute-done | bytes 262176 | tf_op jit(solution)/shard_map/ppermute | solution.py:48
  117.9 3.7 %collective-permute-done.23.rest_7_ = bf16[2,256,256]{2,1,0:T(8,128)(2,1)S(1)} collective-permute-done((bf16[2,256,256]{2,1,0:T(8,128)(2,1)S(1)}, bf16[2,256,256]{2,1,0:T(8,128)(2,1)S(1)}, u32[]{:S(2)}, u32[]{:S(2)}) %collective-permute-start.23) | collective-permute-done | bytes 262176 | tf_op jit(solution)/shard_map/ppermute | solution.py:48
  123.9 10.8 %collective-permute-start.25 = (bf16[2,256,256]{2,1,0:T(8,128)(2,1)S(1)}, bf16[2,256,256]{2,1,0:T(8,128)(2,1)S(1)}, u32[]{:S(2)}, u32[]{:S(2)}) collective-permute-start(bf16[2,256,256]{2,1,0:T(8,128)(2,1)S(1)} %get-tuple-element.94), channel_id=1, source_target_pairs={{0,2},{1,3},{2,0},{3,1},{4,6},{5,7},{6,4},{7,5},{8,10},{9,11},{10,... | collective-permute-start | bytes 786440 | tf_op jit(solution)/shard_map/ppermute | solution.py:48
  134.7 2.0 %collective-permute-start.28 = (bf16[2,256,256]{2,1,0:T(8,128)(2,1)S(1)}, bf16[2,256,256]{2,1,0:T(8,128)(2,1)S(1)}, u32[]{:S(2)}, u32[]{:S(2)}) collective-permute-start(bf16[2,256,256]{2,1,0:T(8,128)(2,1)S(1)} %get-tuple-element.100), channel_id=1, source_target_pairs={{0,1},{1,2},{2,3},{3,0},{4,5},{5,6},{6,7},{7,4},{8,9},{9,10},{10,1... | collective-permute-start | bytes 786440 | tf_op jit(solution)/shard_map/ppermute | solution.py:48
  137.9 1.8 %collective-permute-done.24.rest_1_ = bf16[2,256,256]{2,1,0:T(8,128)(2,1)S(1)} collective-permute-done((bf16[2,256,256]{2,1,0:T(8,128)(2,1)S(1)}, bf16[2,256,256]{2,1,0:T(8,128)(2,1)S(1)}, u32[]{:S(2)}, u32[]{:S(2)}) %collective-permute-start.24) | collective-permute-done | bytes 262176 | tf_op jit(solution)/shard_map/ppermute | solution.py:48
  139.8 8.8 %collective-permute-start.30 = (bf16[2,256,256]{2,1,0:T(8,128)(2,1)S(1)}, bf16[2,256,256]{2,1,0:T(8,128)(2,1)S(1)}, u32[]{:S(2)}, u32[]{:S(2)}) collective-permute-start(bf16[2,256,256]{2,1,0:T(8,128)(2,1)S(1)} %get-tuple-element.102), channel_id=1, source_target_pairs={{0,3},{1,0},{2,1},{3,2},{4,7},{5,4},{6,5},{7,6},{8,11},{9,8},{10,9... | collective-permute-start | bytes 786440 | tf_op jit(solution)/shard_map/ppermute | solution.py:48
  150.1 1.9 %collective-permute-start.27 = (bf16[2,256,256]{2,1,0:T(8,128)(2,1)S(1)}, bf16[2,256,256]{2,1,0:T(8,128)(2,1)S(1)}, u32[]{:S(2)}, u32[]{:S(2)}) collective-permute-start(bf16[2,256,256]{2,1,0:T(8,128)(2,1)S(1)} %get-tuple-element.97), channel_id=1, source_target_pairs={{0,4},{4,8},{8,12},{12,16},{16,20},{20,24},{24,28},{28,32},{32,36}... | collective-permute-start | bytes 786440 | tf_op jit(solution)/shard_map/ppermute | solution.py:54
  153.2 5.2 %collective-permute-done.30.rest_3_ = bf16[2,256,256]{2,1,0:T(8,128)(2,1)S(1)} collective-permute-done((bf16[2,256,256]{2,1,0:T(8,128)(2,1)S(1)}, bf16[2,256,256]{2,1,0:T(8,128)(2,1)S(1)}, u32[]{:S(2)}, u32[]{:S(2)}) %collective-permute-start.30) | collective-permute-done | bytes 262176 | tf_op jit(solution)/shard_map/ppermute | solution.py:48
  159.9 1.9 %collective-permute-start.31 = (bf16[2,256,256]{2,1,0:T(8,128)(2,1)S(1)}, bf16[2,256,256]{2,1,0:T(8,128)(2,1)S(1)}, u32[]{:S(2)}, u32[]{:S(2)}) collective-permute-start(bf16[2,256,256]{2,1,0:T(8,128)(2,1)S(1)} %get-tuple-element.104), channel_id=1, source_target_pairs={{0,4},{4,8},{8,12},{12,16},{16,20},{20,24},{24,28},{28,32},{32,36}... | collective-permute-start | bytes 786440 | tf_op jit(solution)/shard_map/ppermute | solution.py:54
  161.8 7.9 %collective-permute-done.31.rest_5_ = bf16[2,256,256]{2,1,0:T(8,128)(2,1)S(1)} collective-permute-done((bf16[2,256,256]{2,1,0:T(8,128)(2,1)S(1)}, bf16[2,256,256]{2,1,0:T(8,128)(2,1)S(1)}, u32[]{:S(2)}, u32[]{:S(2)}) %collective-permute-start.31) | collective-permute-done | bytes 262176 | tf_op jit(solution)/shard_map/ppermute | solution.py:54
  (78 shorter events, 40.6 us)
Async XLA Ops:
  2.2 11.0 %collective-permute-start = (bf16[2,256,256]{2,1,0:T(8,128)(2,1)S(1)}, bf16[2,256,256]{2,1,0:T(8,128)(2,1)S(1)}, u32[]{:S(2)}, u32[]{:S(2)}) collective-permute-start(bf16[2,256,256]{2,1,0:T(8,128)(2,1)S(1)} %get-tuple-element.106), channel_id=1, source_target_pairs={{4,0},{8,4},{12,8},{16,12},{20,16},{24,20},{28,24},{32,28},{36,32}... | collective-permute-start | bytes 786440 | tf_op jit(solution)/shard_map/ppermute | solution.py:54
  9.3 10.1 %collective-permute-start.4 = (bf16[2,256,256]{2,1,0:T(8,128)(2,1)}, bf16[2,256,256]{2,1,0:T(8,128)(2,1)S(1)}, u32[]{:S(2)}, u32[]{:S(2)}) collective-permute-start(bf16[2,256,256]{2,1,0:T(8,128)(2,1)} %get-tuple-element.105), channel_id=1, source_target_pairs={{4,0},{8,4},{12,8},{16,12},{20,16},{24,20},{28,24},{32,28},{36,32}... | collective-permute-start | bytes 786440 | tf_op jit(solution)/shard_map/ppermute | solution.py:54
  14.6 12.1 %collective-permute-start.1 = (bf16[2,256,256]{2,1,0:T(8,128)(2,1)S(1)}, bf16[2,256,256]{2,1,0:T(8,128)(2,1)S(1)}, u32[]{:S(2)}, u32[]{:S(2)}) collective-permute-start(bf16[2,256,256]{2,1,0:T(8,128)(2,1)S(1)} %get-tuple-element.58), channel_id=1, source_target_pairs={{0,1},{1,2},{2,3},{3,0},{4,5},{5,6},{6,7},{7,4},{8,9},{9,10},{10,1... | collective-permute-start | bytes 786440 | tf_op jit(solution)/shard_map/ppermute | solution.py:48
  16.1 12.5 %collective-permute-start.2 = (bf16[2,256,256]{2,1,0:T(8,128)(2,1)}, bf16[2,256,256]{2,1,0:T(8,128)(2,1)S(1)}, u32[]{:S(2)}, u32[]{:S(2)}) collective-permute-start(bf16[2,256,256]{2,1,0:T(8,128)(2,1)} %get-tuple-element.59), channel_id=1, source_target_pairs={{0,2},{1,3},{2,0},{3,1},{4,6},{5,7},{6,4},{7,5},{8,10},{9,11},{10,... | collective-permute-start | bytes 786440 | tf_op jit(solution)/shard_map/ppermute | solution.py:48
  17.2 15.6 %collective-permute-start.3 = (bf16[2,256,256]{2,1,0:T(8,128)(2,1)}, bf16[2,256,256]{2,1,0:T(8,128)(2,1)}, u32[]{:S(2)}, u32[]{:S(2)}) collective-permute-start(bf16[2,256,256]{2,1,0:T(8,128)(2,1)} %get-tuple-element.60), channel_id=1, source_target_pairs={{0,3},{1,0},{2,1},{3,2},{4,7},{5,4},{6,5},{7,6},{8,11},{9,8},{10,9... | collective-permute-start | bytes 786440 | tf_op jit(solution)/shard_map/ppermute | solution.py:48
  21.6 13.6 %collective-permute-start.5 = (bf16[2,256,256]{2,1,0:T(8,128)(2,1)}, bf16[2,256,256]{2,1,0:T(8,128)(2,1)}, u32[]{:S(2)}, u32[]{:S(2)}) collective-permute-start(bf16[2,256,256]{2,1,0:T(8,128)(2,1)} %get-tuple-element.62), channel_id=1, source_target_pairs={{0,1},{1,2},{2,3},{3,0},{4,5},{5,6},{6,7},{7,4},{8,9},{9,10},{10,1... | collective-permute-start | bytes 786440 | tf_op jit(solution)/shard_map/ppermute | solution.py:48
  21.6 16.8 %collective-permute-start.6 = (bf16[2,256,256]{2,1,0:T(8,128)(2,1)}, bf16[2,256,256]{2,1,0:T(8,128)(2,1)}, u32[]{:S(2)}, u32[]{:S(2)}) collective-permute-start(bf16[2,256,256]{2,1,0:T(8,128)(2,1)} %get-tuple-element.63), channel_id=1, source_target_pairs={{0,2},{1,3},{2,0},{3,1},{4,6},{5,7},{6,4},{7,5},{8,10},{9,11},{10,... | collective-permute-start | bytes 786440 | tf_op jit(solution)/shard_map/ppermute | solution.py:48
  26.7 14.6 %collective-permute-start.7 = (bf16[2,256,256]{2,1,0:T(8,128)(2,1)}, bf16[2,256,256]{2,1,0:T(8,128)(2,1)}, u32[]{:S(2)}, u32[]{:S(2)}) collective-permute-start(bf16[2,256,256]{2,1,0:T(8,128)(2,1)} %get-tuple-element.64), channel_id=1, source_target_pairs={{0,3},{1,0},{2,1},{3,2},{4,7},{5,4},{6,5},{7,6},{8,11},{9,8},{10,9... | collective-permute-start | bytes 786440 | tf_op jit(solution)/shard_map/ppermute | solution.py:48
  47.3 15.5 %collective-permute-start.8 = (bf16[2,256,256]{2,1,0:T(8,128)(2,1)}, bf16[2,256,256]{2,1,0:T(8,128)(2,1)S(1)}, u32[]{:S(2)}, u32[]{:S(2)}) collective-permute-start(bf16[2,256,256]{2,1,0:T(8,128)(2,1)} %get-tuple-element.66), channel_id=1, source_target_pairs={{0,1},{1,2},{2,3},{3,0},{4,5},{5,6},{6,7},{7,4},{8,9},{9,10},{10,1... | collective-permute-start | bytes 786440 | tf_op jit(solution)/shard_map/ppermute | solution.py:48
  48.6 23.6 %collective-permute-start.9 = (bf16[2,256,256]{2,1,0:T(8,128)(2,1)}, bf16[2,256,256]{2,1,0:T(8,128)(2,1)S(1)}, u32[]{:S(2)}, u32[]{:S(2)}) collective-permute-start(bf16[2,256,256]{2,1,0:T(8,128)(2,1)} %get-tuple-element.67), channel_id=1, source_target_pairs={{0,2},{1,3},{2,0},{3,1},{4,6},{5,7},{6,4},{7,5},{8,10},{9,11},{10,... | collective-permute-start | bytes 786440 | tf_op jit(solution)/shard_map/ppermute | solution.py:48
  58.7 13.7 %collective-permute-start.10 = (bf16[2,256,256]{2,1,0:T(8,128)(2,1)}, bf16[2,256,256]{2,1,0:T(8,128)(2,1)S(1)}, u32[]{:S(2)}, u32[]{:S(2)}) collective-permute-start(bf16[2,256,256]{2,1,0:T(8,128)(2,1)} %get-tuple-element.68), channel_id=1, source_target_pairs={{0,3},{1,0},{2,1},{3,2},{4,7},{5,4},{6,5},{7,6},{8,11},{9,8},{10,9... | collective-permute-start | bytes 786440 | tf_op jit(solution)/shard_map/ppermute | solution.py:48
  59.3 21.4 %collective-permute-start.13 = (bf16[2,256,256]{2,1,0:T(8,128)(2,1)}, bf16[2,256,256]{2,1,0:T(8,128)(2,1)S(1)}, u32[]{:S(2)}, u32[]{:S(2)}) collective-permute-start(bf16[2,256,256]{2,1,0:T(8,128)(2,1)} %copy-done.12), channel_id=1, source_target_pairs={{0,1},{1,2},{2,3},{3,0},{4,5},{5,6},{6,7},{7,4},{8,9},{9,10},{10,1... | collective-permute-start | bytes 786440 | tf_op jit(solution)/shard_map/ppermute | solution.py:48
  61.4 19.4 %collective-permute-start.14 = (bf16[2,256,256]{2,1,0:T(8,128)(2,1)}, bf16[2,256,256]{2,1,0:T(8,128)(2,1)S(1)}, u32[]{:S(2)}, u32[]{:S(2)}) collective-permute-start(bf16[2,256,256]{2,1,0:T(8,128)(2,1)} %copy-done.11), channel_id=1, source_target_pairs={{0,2},{1,3},{2,0},{3,1},{4,6},{5,7},{6,4},{7,5},{8,10},{9,11},{10,... | collective-permute-start | bytes 786440 | tf_op jit(solution)/shard_map/ppermute | solution.py:48
  62.8 20.1 %collective-permute-start.15 = (bf16[2,256,256]{2,1,0:T(8,128)(2,1)}, bf16[2,256,256]{2,1,0:T(8,128)(2,1)S(1)}, u32[]{:S(2)}, u32[]{:S(2)}) collective-permute-start(bf16[2,256,256]{2,1,0:T(8,128)(2,1)} %copy-done.10), channel_id=1, source_target_pairs={{0,3},{1,0},{2,1},{3,2},{4,7},{5,4},{6,5},{7,6},{8,11},{9,8},{10,9... | collective-permute-start | bytes 786440 | tf_op jit(solution)/shard_map/ppermute | solution.py:48
  74.3 8.6 %collective-permute-start.12 = (bf16[2,256,256]{2,1,0:T(8,128)(2,1)S(1)}, bf16[2,256,256]{2,1,0:T(8,128)(2,1)S(1)}, u32[]{:S(2)}, u32[]{:S(2)}) collective-permute-start(bf16[2,256,256]{2,1,0:T(8,128)(2,1)S(1)} %get-tuple-element.71), channel_id=1, source_target_pairs={{4,0},{8,4},{12,8},{16,12},{20,16},{24,20},{28,24},{32,28},{36,32}... | collective-permute-start | bytes 786440 | tf_op jit(solution)/shard_map/ppermute | solution.py:54
  78.8 9.8 %collective-permute-start.11 = (bf16[2,256,256]{2,1,0:T(8,128)(2,1)S(1)}, bf16[2,256,256]{2,1,0:T(8,128)(2,1)S(1)}, u32[]{:S(2)}, u32[]{:S(2)}) collective-permute-start(bf16[2,256,256]{2,1,0:T(8,128)(2,1)S(1)} %get-tuple-element.70.rest_3_), channel_id=1, source_target_pairs={{0,4},{4,8},{8,12},{12,16},{16,20},{20,24},{24,28},{28,32},{32,36}... | collective-permute-start | bytes 786440 | tf_op jit(solution)/shard_map/ppermute | solution.py:54
  90.8 8.3 %collective-permute-start.20 = (bf16[2,256,256]{2,1,0:T(8,128)(2,1)S(1)}, bf16[2,256,256]{2,1,0:T(8,128)(2,1)S(1)}, u32[]{:S(2)}, u32[]{:S(2)}) collective-permute-start(bf16[2,256,256]{2,1,0:T(8,128)(2,1)S(1)} %get-tuple-element.87), channel_id=1, source_target_pairs={{4,0},{8,4},{12,8},{16,12},{20,16},{24,20},{28,24},{32,28},{36,32}... | collective-permute-start | bytes 786440 | tf_op jit(solution)/shard_map/ppermute | solution.py:54
  92.8 9.8 %collective-permute-start.19 = (bf16[2,256,256]{2,1,0:T(8,128)(2,1)S(1)}, bf16[2,256,256]{2,1,0:T(8,128)(2,1)S(1)}, u32[]{:S(2)}, u32[]{:S(2)}) collective-permute-start(bf16[2,256,256]{2,1,0:T(8,128)(2,1)S(1)} %get-tuple-element.86.spill_ref), channel_id=1, source_target_pairs={{0,4},{4,8},{8,12},{12,16},{16,20},{20,24},{24,28},{28,32},{32,36}... | collective-permute-start | bytes 786440 | tf_op jit(solution)/shard_map/ppermute | solution.py:54
  95.2 10.1 %collective-permute-start.16 = (bf16[2,256,256]{2,1,0:T(8,128)(2,1)S(1)}, bf16[2,256,256]{2,1,0:T(8,128)(2,1)S(1)}, u32[]{:S(2)}, u32[]{:S(2)}) collective-permute-start(bf16[2,256,256]{2,1,0:T(8,128)(2,1)S(1)} %get-tuple-element.82), channel_id=1, source_target_pairs={{0,1},{1,2},{2,3},{3,0},{4,5},{5,6},{6,7},{7,4},{8,9},{9,10},{10,1... | collective-permute-start | bytes 786440 | tf_op jit(solution)/shard_map/ppermute | solution.py:48
  96.0 12.5 %collective-permute-start.17 = (bf16[2,256,256]{2,1,0:T(8,128)(2,1)S(1)}, bf16[2,256,256]{2,1,0:T(8,128)(2,1)S(1)}, u32[]{:S(2)}, u32[]{:S(2)}) collective-permute-start(bf16[2,256,256]{2,1,0:T(8,128)(2,1)S(1)} %get-tuple-element.83), channel_id=1, source_target_pairs={{0,2},{1,3},{2,0},{3,1},{4,6},{5,7},{6,4},{7,5},{8,10},{9,11},{10,... | collective-permute-start | bytes 786440 | tf_op jit(solution)/shard_map/ppermute | solution.py:48
  97.1 15.3 %collective-permute-start.18 = (bf16[2,256,256]{2,1,0:T(8,128)(2,1)S(1)}, bf16[2,256,256]{2,1,0:T(8,128)(2,1)S(1)}, u32[]{:S(2)}, u32[]{:S(2)}) collective-permute-start(bf16[2,256,256]{2,1,0:T(8,128)(2,1)S(1)} %get-tuple-element.84), channel_id=1, source_target_pairs={{0,3},{1,0},{2,1},{3,2},{4,7},{5,4},{6,5},{7,6},{8,11},{9,8},{10,9... | collective-permute-start | bytes 786440 | tf_op jit(solution)/shard_map/ppermute | solution.py:48
  103.4 12.3 %collective-permute-start.21 = (bf16[2,256,256]{2,1,0:T(8,128)(2,1)S(1)}, bf16[2,256,256]{2,1,0:T(8,128)(2,1)S(1)}, u32[]{:S(2)}, u32[]{:S(2)}) collective-permute-start(bf16[2,256,256]{2,1,0:T(8,128)(2,1)S(1)} %get-tuple-element.89), channel_id=1, source_target_pairs={{0,1},{1,2},{2,3},{3,0},{4,5},{5,6},{6,7},{7,4},{8,9},{9,10},{10,1... | collective-permute-start | bytes 786440 | tf_op jit(solution)/shard_map/ppermute | solution.py:48
  104.2 13.7 %collective-permute-start.22 = (bf16[2,256,256]{2,1,0:T(8,128)(2,1)S(1)}, bf16[2,256,256]{2,1,0:T(8,128)(2,1)S(1)}, u32[]{:S(2)}, u32[]{:S(2)}) collective-permute-start(bf16[2,256,256]{2,1,0:T(8,128)(2,1)S(1)} %get-tuple-element.90), channel_id=1, source_target_pairs={{0,2},{1,3},{2,0},{3,1},{4,6},{5,7},{6,4},{7,5},{8,10},{9,11},{10,... | collective-permute-start | bytes 786440 | tf_op jit(solution)/shard_map/ppermute | solution.py:48
  105.3 16.3 %collective-permute-start.23 = (bf16[2,256,256]{2,1,0:T(8,128)(2,1)S(1)}, bf16[2,256,256]{2,1,0:T(8,128)(2,1)S(1)}, u32[]{:S(2)}, u32[]{:S(2)}) collective-permute-start(bf16[2,256,256]{2,1,0:T(8,128)(2,1)S(1)} %get-tuple-element.91), channel_id=1, source_target_pairs={{0,3},{1,0},{2,1},{3,2},{4,7},{5,4},{6,5},{7,6},{8,11},{9,8},{10,9... | collective-permute-start | bytes 786440 | tf_op jit(solution)/shard_map/ppermute | solution.py:48
  122.5 17.3 %collective-permute-start.24 = (bf16[2,256,256]{2,1,0:T(8,128)(2,1)S(1)}, bf16[2,256,256]{2,1,0:T(8,128)(2,1)S(1)}, u32[]{:S(2)}, u32[]{:S(2)}) collective-permute-start(bf16[2,256,256]{2,1,0:T(8,128)(2,1)S(1)} %get-tuple-element.93), channel_id=1, source_target_pairs={{0,1},{1,2},{2,3},{3,0},{4,5},{5,6},{6,7},{7,4},{8,9},{9,10},{10,1... | collective-permute-start | bytes 786440 | tf_op jit(solution)/shard_map/ppermute | solution.py:48
  123.9 24.7 %collective-permute-start.25 = (bf16[2,256,256]{2,1,0:T(8,128)(2,1)S(1)}, bf16[2,256,256]{2,1,0:T(8,128)(2,1)S(1)}, u32[]{:S(2)}, u32[]{:S(2)}) collective-permute-start(bf16[2,256,256]{2,1,0:T(8,128)(2,1)S(1)} %get-tuple-element.94), channel_id=1, source_target_pairs={{0,2},{1,3},{2,0},{3,1},{4,6},{5,7},{6,4},{7,5},{8,10},{9,11},{10,... | collective-permute-start | bytes 786440 | tf_op jit(solution)/shard_map/ppermute | solution.py:48
  134.7 13.9 %collective-permute-start.26 = (bf16[2,256,256]{2,1,0:T(8,128)(2,1)S(1)}, bf16[2,256,256]{2,1,0:T(8,128)(2,1)S(1)}, u32[]{:S(2)}, u32[]{:S(2)}) collective-permute-start(bf16[2,256,256]{2,1,0:T(8,128)(2,1)S(1)} %get-tuple-element.95), channel_id=1, source_target_pairs={{0,3},{1,0},{2,1},{3,2},{4,7},{5,4},{6,5},{7,6},{8,11},{9,8},{10,9... | collective-permute-start | bytes 786440 | tf_op jit(solution)/shard_map/ppermute | solution.py:48
  134.7 17.4 %collective-permute-start.28 = (bf16[2,256,256]{2,1,0:T(8,128)(2,1)S(1)}, bf16[2,256,256]{2,1,0:T(8,128)(2,1)S(1)}, u32[]{:S(2)}, u32[]{:S(2)}) collective-permute-start(bf16[2,256,256]{2,1,0:T(8,128)(2,1)S(1)} %get-tuple-element.100), channel_id=1, source_target_pairs={{0,1},{1,2},{2,3},{3,0},{4,5},{5,6},{6,7},{7,4},{8,9},{9,10},{10,1... | collective-permute-start | bytes 786440 | tf_op jit(solution)/shard_map/ppermute | solution.py:48
  136.7 16.5 %collective-permute-start.29 = (bf16[2,256,256]{2,1,0:T(8,128)(2,1)S(1)}, bf16[2,256,256]{2,1,0:T(8,128)(2,1)S(1)}, u32[]{:S(2)}, u32[]{:S(2)}) collective-permute-start(bf16[2,256,256]{2,1,0:T(8,128)(2,1)S(1)} %get-tuple-element.101), channel_id=1, source_target_pairs={{0,2},{1,3},{2,0},{3,1},{4,6},{5,7},{6,4},{7,5},{8,10},{9,11},{10,... | collective-permute-start | bytes 786440 | tf_op jit(solution)/shard_map/ppermute | solution.py:48
  139.8 18.6 %collective-permute-start.30 = (bf16[2,256,256]{2,1,0:T(8,128)(2,1)S(1)}, bf16[2,256,256]{2,1,0:T(8,128)(2,1)S(1)}, u32[]{:S(2)}, u32[]{:S(2)}) collective-permute-start(bf16[2,256,256]{2,1,0:T(8,128)(2,1)S(1)} %get-tuple-element.102), channel_id=1, source_target_pairs={{0,3},{1,0},{2,1},{3,2},{4,7},{5,4},{6,5},{7,6},{8,11},{9,8},{10,9... | collective-permute-start | bytes 786440 | tf_op jit(solution)/shard_map/ppermute | solution.py:48
  150.1 11.6 %collective-permute-start.27 = (bf16[2,256,256]{2,1,0:T(8,128)(2,1)S(1)}, bf16[2,256,256]{2,1,0:T(8,128)(2,1)S(1)}, u32[]{:S(2)}, u32[]{:S(2)}) collective-permute-start(bf16[2,256,256]{2,1,0:T(8,128)(2,1)S(1)} %get-tuple-element.97), channel_id=1, source_target_pairs={{0,4},{4,8},{8,12},{12,16},{16,20},{20,24},{24,28},{28,32},{32,36}... | collective-permute-start | bytes 786440 | tf_op jit(solution)/shard_map/ppermute | solution.py:54
  159.9 9.8 %collective-permute-start.31 = (bf16[2,256,256]{2,1,0:T(8,128)(2,1)S(1)}, bf16[2,256,256]{2,1,0:T(8,128)(2,1)S(1)}, u32[]{:S(2)}, u32[]{:S(2)}) collective-permute-start(bf16[2,256,256]{2,1,0:T(8,128)(2,1)S(1)} %get-tuple-element.104), channel_id=1, source_target_pairs={{0,4},{4,8},{8,12},{12,16},{16,20},{20,24},{24,28},{28,32},{32,36}... | collective-permute-start | bytes 786440 | tf_op jit(solution)/shard_map/ppermute | solution.py:54
  (13 other events, 87.0 us)
where the time goes:
time: 173 us; the launch traced here: 171 us
  starting transfers between devices  88.7 us (51%)
  waiting for transfers between devices  55.7 us (32%)
  Pallas kernels  14.8 us (9%)
  local copies, waits for them, and re-layouts  9.07 us (5%)
    ppermute x24, starting transfers between devices, shift(): lax.ppermute(block, axis, [(i, (i + distance) % size) for i in range(size)])  64.5 us
    ppermute x24, waiting for transfers between devices, shift(): lax.ppermute(block, axis, [(i, (i + distance) % size) for i in range(size)])  38 us
    ppermute x8, starting transfers between devices, step(): return lax.ppermute(block, axis, route)  24.3 us
    ppermute x8, waiting for transfers between devices, step(): return lax.ppermute(block, axis, route)  17.6 us
    unnamed x26, local copies, waits for them, and re-layouts  7.06 us
    pallas_call x3, Pallas kernels, add_up(): pl.pallas_call(sum_part, compiler_params=limit(SMALL), out_shape=[plane32...  4 us
  transfers between devices with their start and end apart: 32, of which 19 were waited for; matrix products, arithmetic and copies ran while one was open for 1% of the time, Pallas kernels for 6%

commit v1 on v0

--- a/solution.py
+++ b/solution.py
@@ -54,6 +54,11 @@
     return lax.ppermute(block, axis, route)
 
 
+def offset_at(offsets_ref, distance):
+    cut = lax.axis_index("cuts").astype(jnp.int32)
+    return offsets_ref[lax.rem(cut + distance + CUTS, CUTS)]
+
+
 def chunks(size):
     for m in range(0, PAT, size):
         yield pl.ds(m, size), m + lax.broadcasted_iota(jnp.int32, (size, PAT), 0)
@@ -61,7 +66,12 @@
 
 def cut_windows(own, margin, rows, place, offsets_ref, outs, j):
     for d in range(CUTS):
-        outs[d][j, place] = jnp.where(rows >= offsets_ref[d], own, margin).astype(bf16)
+        outs[d][j, place] = jnp.where(rows >= offset_at(offsets_ref, d), own, margin).astype(bf16)
+
+
+def cast_kernel(own_ref, *outs):
+    for i in range(LOCAL):
+        outs[i][...] = own_ref[i].astype(bf16)
 
 
 def pack_kernel(i, offsets_ref, own_ref, margin_ref, *outs):
@@ -90,7 +100,7 @@
             own, spill = 0.0, 0.0
             for d in range(CUTS):
                 part = parts[d][j, place].astype(f32)
-                here = rows >= offsets_ref[d]
+                here = rows >= offset_at(offsets_ref, -d)
                 own = own + jnp.where(here, part, 0.0)
                 spill = spill + jnp.where(here, 0.0, part)
             sum_ref[j, place] = own
@@ -98,10 +108,10 @@
             spill_ref[j, place] = spill.astype(bf16)
 
 
-def middle_kernel(ahead_ref, behind_ref, *rest):
+def middle_kernel(offsets_ref, *rest):
     ins, outs = rest[: 6 + CUTS], rest[6 + CUTS :]
-    update_part(0, ahead_ref, *ins[:6], *outs[: 1 + CUTS])
-    sum_part(behind_ref, *ins[6:], *outs[1 + CUTS :])
+    update_part(0, offsets_ref, *ins[:6], *outs[: 1 + CUTS])
+    sum_part(offsets_ref, *ins[6:], *outs[1 + CUTS :])
 
 
 def finish_kernel(*rest):
@@ -112,8 +122,8 @@
         new_ref[i] = own_ref[...] - object_rate * arrived
 
 
-def prepare_kernel(scalars_ref, tables_ref, probe_ref, mats_ref, start_ref):
-    turn = scalars_ref[2]
+def prepare_kernel(offsets_ref, tables_ref, probe_ref, mats_ref, start_ref):
+    turn = offset_at(offsets_ref, 0)
 
     def put(m, re, im):
         mats_ref[m, :PAT, :PAT] = re
@@ -146,12 +156,12 @@
     ]
 
 
-def slot_kernel(scalars_ref, mats, start_ref, amplitudes_ref, *rest):
+def slot_kernel(counts_ref, mats, start_ref, amplitudes_ref, *rest):
     count = CUTS * LOCAL
     sources, results = rest[:count], rest[count : 2 * count]
     window, saved, terms, field, inner, amplitude, in_sem, out_sem, side_sem = rest[2 * count :]
-    cut = scalars_ref[0]
-    live = scalars_ref[1]
+    cut = lax.axis_index("cuts").astype(jnp.int32)
+    live = (cut < counts_ref[0]).astype(jnp.int32)
 
     @pl.when(live == 0)
     def _():
@@ -283,6 +293,16 @@
     return pltpu.with_memory_space_constraint(array, pltpu.MemorySpace.HBM)
 
 
+def cast(own):
+    return pl.pallas_call(
+        cast_kernel,
+        compiler_params=limit(SMALL),
+        out_shape=[plane16] * LOCAL,
+        in_specs=vmem(1),
+        out_specs=vmem(LOCAL),
+    )(own)
+
+
 def pack(i, offsets, own, margin):
     return pl.pallas_call(
         partial(pack_kernel, i),
@@ -313,14 +333,14 @@
     )(offsets, *parts)
 
 
-def middle(ahead, behind, *arrays):
+def middle(offsets, *arrays):
     return pl.pallas_call(
         middle_kernel,
         compiler_params=limit(SMALL),
         out_shape=[plane32] + [plane16] * CUTS + [plane32, plane16, plane16],
-        in_specs=smem(2) + vmem(6 + CUTS),
+        in_specs=smem() + vmem(6 + CUTS),
         out_specs=vmem(4 + CUTS),
-    )(ahead, behind, *arrays)
+    )(offsets, *arrays)
 
 
 def finish(*arrays):
@@ -329,7 +349,7 @@
     )(*arrays)
 
 
-def prepare(scalars, tabs, probe):
+def prepare(offsets, tabs, probe):
     return pl.pallas_call(
         prepare_kernel,
         compiler_params=limit(SMALL),
@@ -339,10 +359,10 @@
         ],
         in_specs=smem() + vmem(2),
         out_specs=vmem(2),
-    )(scalars, tabs, probe)
-
-
-def run_slot(scalars, mats, start, amplitudes, windows):
+    )(offsets, tabs, probe)
+
+
+def run_slot(counts, mats, start, amplitudes, windows):
     count = CUTS * LOCAL
     return pl.pallas_call(
         slot_kernel,
@@ -363,7 +383,7 @@
             pltpu.SemaphoreType.DMA((count,)),
             pltpu.SemaphoreType.DMA,
         ],
-    )(scalars, mats, start, in_hbm(amplitudes), *windows)
+    )(counts, mats, start, in_hbm(amplitudes), *windows)
 
 
 def exchange(blocks):
@@ -375,27 +395,21 @@
 
 def run(object_slices, probe_field, row_offsets, columns, counts, amplitudes):
     tabs = jnp.asarray(tables(PAT))
-    cut = lax.axis_index("cuts").astype(jnp.int32)
-    turn = jnp.arange(CUTS, dtype=jnp.int32)
-    ahead = row_offsets[(cut + turn) % CUTS]
-    behind = row_offsets[(cut - turn + CUTS) % CUTS]
-    live = (cut < counts[0]).astype(jnp.int32)
-    scalars = jnp.stack([cut, live, ahead[0]])
-    constants = prepare(scalars, tabs, probe_field)
+    constants = prepare(row_offsets, tabs, probe_field)
     each = range(LOCAL)
-    margins = [step(object_slices[i].astype(bf16), "tile", -1) for i in each]
+    margins = [step(rows, "tile", -1) for rows in cast(object_slices)]
     windows = []
     for i in each:
-        windows += exchange(pack(i, ahead, object_slices, margins[i]))
+        windows += exchange(pack(i, row_offsets, object_slices, margins[i]))
     for iteration in range(ITERS):
-        terms = run_slot(scalars, *constants, amplitudes, windows)
+        terms = run_slot(counts, *constants, amplitudes, windows)
         first, second = (exchange(terms[CUTS * i : CUTS * (i + 1)]) for i in each)
-        total_a, total16_a, spill_a = add_up(behind, first)
+        total_a, total16_a, spill_a = add_up(row_offsets, first)
         spill_in_a = step(spill_a, "tile", 1)
         if iteration + 1 < ITERS:
             total_in_a = step(total16_a, "tile", -1)
             out = middle(
-                ahead, behind, object_slices, margins[0], total_a, spill_a, spill_in_a,
+                row_offsets, object_slices, margins[0], total_a, spill_a, spill_in_a,
                 total_in_a, *second
             )
             own_a, cut_a, (total_b, total16_b, spill_b) = out[0], out[1 : 1 + CUTS], out[1 + CUTS :]
@@ -403,12 +417,10 @@
             total_in_b = step(total16_b, "tile", -1)
             windows = exchange(cut_a)
             own_b, *cut_b = update(
-                1, ahead, object_slices, margins[1], total_b, spill_b, spill_in_b, total_in_b
+                1, row_offsets, object_slices, margins[1], total_b, spill_b, spill_in_b, total_in_b
             )
             windows += exchange(cut_b)
-            again, own_a = lax.optimization_barrier((scalars, own_a))
-            constants = prepare(again, tabs, probe_field)
-    total_b, _, spill_b = add_up(behind, second)
+    total_b, _, spill_b = add_up(row_offsets, second)
     spill_in_b = step(spill_b, "tile", 1)
     return finish(own_a, total_a, spill_in_a, own_b, total_b, spill_in_b)
 

time: 173 us -> 163 us (0.942)
  local copies, waits for them, and re-layouts: 9.07 us -> 1.89 us
  Pallas kernels: 14.8 us -> 10.6 us
  waiting for transfers between devices: 55.7 us -> 59.3 us
    unnamed x26 -> x12, local copies, waits for them, and re-layouts: 7.06 us -> 1.89 us
    ppermute x24, waiting for transfers between devices: 38 us -> 40.1 us  [shift(): lax.ppermute(block, axis, [(i, (i + distance) % size) for i in range(size)])]
    pallas_call x2, Pallas kernels: 2.49 us -> 0.66 us  [run_slot(): pl.pallas_call(slot_kernel, compiler_params=limit(LARGE), out_shape=[plan...]
  transfers between devices with their start and end apart: 32 -> 32, of which waited for: 19 -> 19; matrix products, arithmetic and copies ran while one was open for 1% -> 0% of each run, Pallas kernels for 6% -> 5%
where the time goes in v1:
time: 163 us; the launch traced here: 162 us
  starting transfers between devices  89.5 us (55%)
  waiting for transfers between devices  59.3 us (36%)
  Pallas kernels  10.6 us (7%)
  local copies, waits for them, and re-layouts  1.89 us (1%)
    ppermute x24, starting transfers between devices, shift(): lax.ppermute(block, axis, [(i, (i + distance) % size) for i in range(size)])  65.1 us
    ppermute x24, waiting for transfers between devices, shift(): lax.ppermute(block, axis, [(i, (i + distance) % size) for i in range(size)])  40.1 us
    ppermute x8, starting transfers between devices, step(): return lax.ppermute(block, axis, route)  24.4 us
    ppermute x8, waiting for transfers between devices, step(): return lax.ppermute(block, axis, route)  19.2 us
    pallas_call x3, Pallas kernels, add_up(): pl.pallas_call(sum_part, compiler_params=limit(SMALL), out_shape=[plane32...  4.08 us
  transfers between devices with their start and end apart: 32, of which 19 were waited for; matrix products, arithmetic and copies ran while one was open for 0% of the time, Pallas kernels for 5%

profile of v1, /device:TPU:18, one launch (start us, length us, event | category | flops | bytes accessed | tf_op | source)
XLA Modules:
  0.0 162.2 jit_solution(17572099951007668069)
XLA Ops:
  1.3 7.2 %collective-permute-start.4 = (bf16[2,256,256]{2,1,0:T(8,128)(2,1)S(1)}, bf16[2,256,256]{2,1,0:T(8,128)(2,1)S(1)}, u32[]{:S(2)}, u32[]{:S(2)}) collective-permute-start(bf16[2,256,256]{2,1,0:T(8,128)(2,1)S(1)} %get-tuple-element.60), channel_id=1, source_target_pairs={{4,0},{8,4},{12,8},{16,12},{20,16},{24,20},{28,24},{32,28},{36,32}... | collective-permute-start | bytes 786440 | tf_op jit(solution)/shard_map/ppermute | solution.py:54
  8.5 2.6 %collective-permute-start = (bf16[2,256,256]{2,1,0:T(8,128)(2,1)S(1)}, bf16[2,256,256]{2,1,0:T(8,128)(2,1)S(1)}, u32[]{:S(2)}, u32[]{:S(2)}) collective-permute-start(bf16[2,256,256]{2,1,0:T(8,128)(2,1)S(1)} %get-tuple-element.53), channel_id=1, source_target_pairs={{4,0},{8,4},{12,8},{16,12},{20,16},{24,20},{28,24},{32,28},{36,32}... | collective-permute-start | bytes 786440 | tf_op jit(solution)/shard_map/ppermute | solution.py:54
  16.4 2.2 %collective-permute-start.7 = (bf16[2,256,256]{2,1,0:T(8,128)(2,1)S(1)}, bf16[2,256,256]{2,1,0:T(8,128)(2,1)S(1)}, u32[]{:S(2)}, u32[]{:S(2)}) collective-permute-start(bf16[2,256,256]{2,1,0:T(8,128)(2,1)S(1)} %get-tuple-element.64), channel_id=1, source_target_pairs={{0,3},{1,0},{2,1},{3,2},{4,7},{5,4},{6,5},{7,6},{8,11},{9,8},{10,9... | collective-permute-start | bytes 786440 | tf_op jit(solution)/shard_map/ppermute | solution.py:48
  19.4 3.5 %collective-permute-start.2 = (bf16[2,256,256]{2,1,0:T(8,128)(2,1)S(1)}, bf16[2,256,256]{2,1,0:T(8,128)(2,1)S(1)}, u32[]{:S(2)}, u32[]{:S(2)}) collective-permute-start(bf16[2,256,256]{2,1,0:T(8,128)(2,1)S(1)} %get-tuple-element.58), channel_id=1, source_target_pairs={{0,2},{1,3},{2,0},{3,1},{4,6},{5,7},{6,4},{7,5},{8,10},{9,11},{10,... | collective-permute-start | bytes 786440 | tf_op jit(solution)/shard_map/ppermute | solution.py:48
  22.9 4.0 %collective-permute-done.5.rest_5_ = bf16[2,256,256]{2,1,0:T(8,128)(2,1)S(1)} collective-permute-done((bf16[2,256,256]{2,1,0:T(8,128)(2,1)S(1)}, bf16[2,256,256]{2,1,0:T(8,128)(2,1)S(1)}, u32[]{:S(2)}, u32[]{:S(2)}) %collective-permute-start.5) | collective-permute-done | bytes 262176 | tf_op jit(solution)/shard_map/ppermute | solution.py:48
  28.7 3.4 %collective-permute-done.7.rest_7_ = bf16[2,256,256]{2,1,0:T(8,128)(2,1)S(1)} collective-permute-done((bf16[2,256,256]{2,1,0:T(8,128)(2,1)S(1)}, bf16[2,256,256]{2,1,0:T(8,128)(2,1)S(1)}, u32[]{:S(2)}, u32[]{:S(2)}) %collective-permute-start.7) | collective-permute-done | bytes 262176 | tf_op jit(solution)/shard_map/ppermute | solution.py:48
  32.1 2.2 %collective-permute-done.1.rest_1_ = bf16[2,256,256]{2,1,0:T(8,128)(2,1)S(1)} collective-permute-done((bf16[2,256,256]{2,1,0:T(8,128)(2,1)S(1)}, bf16[2,256,256]{2,1,0:T(8,128)(2,1)S(1)}, u32[]{:S(2)}, u32[]{:S(2)}) %collective-permute-start.1) | collective-permute-done | bytes 262176 | tf_op jit(solution)/shard_map/ppermute | solution.py:48
  34.3 3.0 %collective-permute-done.2.rest_2_ = bf16[2,256,256]{2,1,0:T(8,128)(2,1)S(1)} collective-permute-done((bf16[2,256,256]{2,1,0:T(8,128)(2,1)S(1)}, bf16[2,256,256]{2,1,0:T(8,128)(2,1)S(1)}, u32[]{:S(2)}, u32[]{:S(2)}) %collective-permute-start.2) | collective-permute-done | bytes 262176 | tf_op jit(solution)/shard_map/ppermute | solution.py:48
  37.3 2.3 %collective-permute-done.3.rest_3_ = bf16[2,256,256]{2,1,0:T(8,128)(2,1)S(1)} collective-permute-done((bf16[2,256,256]{2,1,0:T(8,128)(2,1)S(1)}, bf16[2,256,256]{2,1,0:T(8,128)(2,1)S(1)}, u32[]{:S(2)}, u32[]{:S(2)}) %collective-permute-start.3) | collective-permute-done | bytes 262176 | tf_op jit(solution)/shard_map/ppermute | solution.py:48
  41.2 10.9 %collective-permute-start.9 = (bf16[2,256,256]{2,1,0:T(8,128)(2,1)S(1)}, bf16[2,256,256]{2,1,0:T(8,128)(2,1)S(1)}, u32[]{:S(2)}, u32[]{:S(2)}) collective-permute-start(bf16[2,256,256]{2,1,0:T(8,128)(2,1)S(1)} %get-tuple-element.67), channel_id=1, source_target_pairs={{0,2},{1,3},{2,0},{3,1},{4,6},{5,7},{6,4},{7,5},{8,10},{9,11},{10,... | collective-permute-start | bytes 786440 | tf_op jit(solution)/shard_map/ppermute | solution.py:48
  52.1 2.0 %collective-permute-start.13 = (bf16[2,256,256]{2,1,0:T(8,128)(2,1)S(1)}, bf16[2,256,256]{2,1,0:T(8,128)(2,1)S(1)}, u32[]{:S(2)}, u32[]{:S(2)}) collective-permute-start(bf16[2,256,256]{2,1,0:T(8,128)(2,1)S(1)} %get-tuple-element.73), channel_id=1, source_target_pairs={{0,1},{1,2},{2,3},{3,0},{4,5},{5,6},{6,7},{7,4},{8,9},{9,10},{10,1... | collective-permute-start | bytes 786440 | tf_op jit(solution)/shard_map/ppermute | solution.py:48
  57.2 9.0 %collective-permute-start.15 = (bf16[2,256,256]{2,1,0:T(8,128)(2,1)S(1)}, bf16[2,256,256]{2,1,0:T(8,128)(2,1)S(1)}, u32[]{:S(2)}, u32[]{:S(2)}) collective-permute-start(bf16[2,256,256]{2,1,0:T(8,128)(2,1)S(1)} %get-tuple-element.75), channel_id=1, source_target_pairs={{0,3},{1,0},{2,1},{3,2},{4,7},{5,4},{6,5},{7,6},{8,11},{9,8},{10,9... | collective-permute-start | bytes 786440 | tf_op jit(solution)/shard_map/ppermute | solution.py:48
  67.2 4.5 %collective-permute-start.12 = (bf16[2,256,256]{2,1,0:T(8,128)(2,1)S(1)}, bf16[2,256,256]{2,1,0:T(8,128)(2,1)S(1)}, u32[]{:S(2)}, u32[]{:S(2)}) collective-permute-start(bf16[2,256,256]{2,1,0:T(8,128)(2,1)S(1)} %get-tuple-element.71), channel_id=1, source_target_pairs={{4,0},{8,4},{12,8},{16,12},{20,16},{24,20},{28,24},{32,28},{36,32}... | collective-permute-start | bytes 786440 | tf_op jit(solution)/shard_map/ppermute | solution.py:54
  71.7 1.9 %collective-permute-start.11 = (bf16[2,256,256]{2,1,0:T(8,128)(2,1)S(1)}, bf16[2,256,256]{2,1,0:T(8,128)(2,1)S(1)}, u32[]{:S(2)}, u32[]{:S(2)}) collective-permute-start(bf16[2,256,256]{2,1,0:T(8,128)(2,1)S(1)} %get-tuple-element.70.rest_3_), channel_id=1, source_target_pairs={{0,4},{4,8},{8,12},{12,16},{16,20},{20,24},{24,28},{28,32},{32,36}... | collective-permute-start | bytes 786440 | tf_op jit(solution)/shard_map/ppermute | solution.py:54
  75.6 5.9 %collective-permute-done.11.rest_4_ = bf16[2,256,256]{2,1,0:T(8,128)(2,1)S(1)} collective-permute-done((bf16[2,256,256]{2,1,0:T(8,128)(2,1)S(1)}, bf16[2,256,256]{2,1,0:T(8,128)(2,1)S(1)}, u32[]{:S(2)}, u32[]{:S(2)}) %collective-permute-start.11) | collective-permute-done | bytes 262176 | tf_op jit(solution)/shard_map/ppermute | solution.py:54
  82.8 1.9 %collective-permute-start.20 = (bf16[2,256,256]{2,1,0:T(8,128)(2,1)S(1)}, bf16[2,256,256]{2,1,0:T(8,128)(2,1)S(1)}, u32[]{:S(2)}, u32[]{:S(2)}) collective-permute-start(bf16[2,256,256]{2,1,0:T(8,128)(2,1)S(1)} %get-tuple-element.83), channel_id=1, source_target_pairs={{4,0},{8,4},{12,8},{16,12},{20,16},{24,20},{28,24},{32,28},{36,32}... | collective-permute-start | bytes 786440 | tf_op jit(solution)/shard_map/ppermute | solution.py:54
  84.7 2.4 %collective-permute-start.19 = (bf16[2,256,256]{2,1,0:T(8,128)(2,1)S(1)}, bf16[2,256,256]{2,1,0:T(8,128)(2,1)S(1)}, u32[]{:S(2)}, u32[]{:S(2)}) collective-permute-start(bf16[2,256,256]{2,1,0:T(8,128)(2,1)S(1)} %get-tuple-element.82.spill_ref), channel_id=1, source_target_pairs={{0,4},{4,8},{8,12},{12,16},{16,20},{20,24},{24,28},{28,32},{32,36}... | collective-permute-start | bytes 786440 | tf_op jit(solution)/shard_map/ppermute | solution.py:54
  87.2 1.9 %collective-permute-start.17 = (bf16[2,256,256]{2,1,0:T(8,128)(2,1)S(1)}, bf16[2,256,256]{2,1,0:T(8,128)(2,1)S(1)}, u32[]{:S(2)}, u32[]{:S(2)}) collective-permute-start(bf16[2,256,256]{2,1,0:T(8,128)(2,1)S(1)} %get-tuple-element.79), channel_id=1, source_target_pairs={{0,2},{1,3},{2,0},{3,1},{4,6},{5,7},{6,4},{7,5},{8,10},{9,11},{10,... | collective-permute-start | bytes 786440 | tf_op jit(solution)/shard_map/ppermute | solution.py:48
  89.1 2.0 %collective-permute-start.18 = (bf16[2,256,256]{2,1,0:T(8,128)(2,1)S(1)}, bf16[2,256,256]{2,1,0:T(8,128)(2,1)S(1)}, u32[]{:S(2)}, u32[]{:S(2)}) collective-permute-start(bf16[2,256,256]{2,1,0:T(8,128)(2,1)S(1)} %get-tuple-element.80), channel_id=1, source_target_pairs={{0,3},{1,0},{2,1},{3,2},{4,7},{5,4},{6,5},{7,6},{8,11},{9,8},{10,9... | collective-permute-start | bytes 786440 | tf_op jit(solution)/shard_map/ppermute | solution.py:48
  91.1 3.5 %collective-permute-done.19.spill_in_ref = bf16[2,256,256]{2,1,0:T(8,128)(2,1)S(1)} collective-permute-done((bf16[2,256,256]{2,1,0:T(8,128)(2,1)S(1)}, bf16[2,256,256]{2,1,0:T(8,128)(2,1)S(1)}, u32[]{:S(2)}, u32[]{:S(2)}) %collective-permute-start.19) | collective-permute-done | bytes 262176 | tf_op jit(solution)/shard_map/ppermute | solution.py:54
  95.5 1.9 %collective-permute-start.22 = (bf16[2,256,256]{2,1,0:T(8,128)(2,1)S(1)}, bf16[2,256,256]{2,1,0:T(8,128)(2,1)S(1)}, u32[]{:S(2)}, u32[]{:S(2)}) collective-permute-start(bf16[2,256,256]{2,1,0:T(8,128)(2,1)S(1)} %get-tuple-element.86), channel_id=1, source_target_pairs={{0,2},{1,3},{2,0},{3,1},{4,6},{5,7},{6,4},{7,5},{8,10},{9,11},{10,... | collective-permute-start | bytes 786440 | tf_op jit(solution)/shard_map/ppermute | solution.py:48
  97.4 2.0 %collective-permute-start.23 = (bf16[2,256,256]{2,1,0:T(8,128)(2,1)S(1)}, bf16[2,256,256]{2,1,0:T(8,128)(2,1)S(1)}, u32[]{:S(2)}, u32[]{:S(2)}) collective-permute-start(bf16[2,256,256]{2,1,0:T(8,128)(2,1)S(1)} %get-tuple-element.87), channel_id=1, source_target_pairs={{0,3},{1,0},{2,1},{3,2},{4,7},{5,4},{6,5},{7,6},{8,11},{9,8},{10,9... | collective-permute-start | bytes 786440 | tf_op jit(solution)/shard_map/ppermute | solution.py:48
  99.3 4.4 %collective-permute-done.18.rest_3_ = bf16[2,256,256]{2,1,0:T(8,128)(2,1)S(1)} collective-permute-done((bf16[2,256,256]{2,1,0:T(8,128)(2,1)S(1)}, bf16[2,256,256]{2,1,0:T(8,128)(2,1)S(1)}, u32[]{:S(2)}, u32[]{:S(2)}) %collective-permute-start.18) | collective-permute-done | bytes 262176 | tf_op jit(solution)/shard_map/ppermute | solution.py:48
  103.7 4.0 %collective-permute-done.21.rest_5_ = bf16[2,256,256]{2,1,0:T(8,128)(2,1)S(1)} collective-permute-done((bf16[2,256,256]{2,1,0:T(8,128)(2,1)S(1)}, bf16[2,256,256]{2,1,0:T(8,128)(2,1)S(1)}, u32[]{:S(2)}, u32[]{:S(2)}) %collective-permute-start.21) | collective-permute-done | bytes 262176 | tf_op jit(solution)/shard_map/ppermute | solution.py:48
  109.3 4.3 %collective-permute-done.23.rest_7_ = bf16[2,256,256]{2,1,0:T(8,128)(2,1)S(1)} collective-permute-done((bf16[2,256,256]{2,1,0:T(8,128)(2,1)S(1)}, bf16[2,256,256]{2,1,0:T(8,128)(2,1)S(1)}, u32[]{:S(2)}, u32[]{:S(2)}) %collective-permute-start.23) | collective-permute-done | bytes 262176 | tf_op jit(solution)/shard_map/ppermute | solution.py:48
  115.0 11.1 %collective-permute-start.25 = (bf16[2,256,256]{2,1,0:T(8,128)(2,1)S(1)}, bf16[2,256,256]{2,1,0:T(8,128)(2,1)S(1)}, u32[]{:S(2)}, u32[]{:S(2)}) collective-permute-start(bf16[2,256,256]{2,1,0:T(8,128)(2,1)S(1)} %get-tuple-element.90), channel_id=1, source_target_pairs={{0,2},{1,3},{2,0},{3,1},{4,6},{5,7},{6,4},{7,5},{8,10},{9,11},{10,... | collective-permute-start | bytes 786440 | tf_op jit(solution)/shard_map/ppermute | solution.py:48
  126.0 2.0 %collective-permute-start.28 = (bf16[2,256,256]{2,1,0:T(8,128)(2,1)S(1)}, bf16[2,256,256]{2,1,0:T(8,128)(2,1)S(1)}, u32[]{:S(2)}, u32[]{:S(2)}) collective-permute-start(bf16[2,256,256]{2,1,0:T(8,128)(2,1)S(1)} %get-tuple-element.96), channel_id=1, source_target_pairs={{0,1},{1,2},{2,3},{3,0},{4,5},{5,6},{6,7},{7,4},{8,9},{9,10},{10,1... | collective-permute-start | bytes 786440 | tf_op jit(solution)/shard_map/ppermute | solution.py:48
  130.9 9.1 %collective-permute-start.30 = (bf16[2,256,256]{2,1,0:T(8,128)(2,1)S(1)}, bf16[2,256,256]{2,1,0:T(8,128)(2,1)S(1)}, u32[]{:S(2)}, u32[]{:S(2)}) collective-permute-start(bf16[2,256,256]{2,1,0:T(8,128)(2,1)S(1)} %get-tuple-element.98), channel_id=1, source_target_pairs={{0,3},{1,0},{2,1},{3,2},{4,7},{5,4},{6,5},{7,6},{8,11},{9,8},{10,9... | collective-permute-start | bytes 786440 | tf_op jit(solution)/shard_map/ppermute | solution.py:48
  141.5 1.9 %collective-permute-start.27 = (bf16[2,256,256]{2,1,0:T(8,128)(2,1)S(1)}, bf16[2,256,256]{2,1,0:T(8,128)(2,1)S(1)}, u32[]{:S(2)}, u32[]{:S(2)}) collective-permute-start(bf16[2,256,256]{2,1,0:T(8,128)(2,1)S(1)} %get-tuple-element.93), channel_id=1, source_target_pairs={{0,4},{4,8},{8,12},{12,16},{16,20},{20,24},{24,28},{28,32},{32,36}... | collective-permute-start | bytes 786440 | tf_op jit(solution)/shard_map/ppermute | solution.py:54
  144.5 5.2 %collective-permute-done.30.rest_3_ = bf16[2,256,256]{2,1,0:T(8,128)(2,1)S(1)} collective-permute-done((bf16[2,256,256]{2,1,0:T(8,128)(2,1)S(1)}, bf16[2,256,256]{2,1,0:T(8,128)(2,1)S(1)}, u32[]{:S(2)}, u32[]{:S(2)}) %collective-permute-start.30) | collective-permute-done | bytes 262176 | tf_op jit(solution)/shard_map/ppermute | solution.py:48
  151.3 1.9 %collective-permute-start.31 = (bf16[2,256,256]{2,1,0:T(8,128)(2,1)S(1)}, bf16[2,256,256]{2,1,0:T(8,128)(2,1)S(1)}, u32[]{:S(2)}, u32[]{:S(2)}) collective-permute-start(bf16[2,256,256]{2,1,0:T(8,128)(2,1)S(1)} %get-tuple-element.100), channel_id=1, source_target_pairs={{0,4},{4,8},{8,12},{12,16},{16,20},{20,24},{24,28},{28,32},{32,36}... | collective-permute-start | bytes 786440 | tf_op jit(solution)/shard_map/ppermute | solution.py:54
  153.2 7.9 %collective-permute-done.31.rest_5_ = bf16[2,256,256]{2,1,0:T(8,128)(2,1)S(1)} collective-permute-done((bf16[2,256,256]{2,1,0:T(8,128)(2,1)S(1)}, bf16[2,256,256]{2,1,0:T(8,128)(2,1)S(1)}, u32[]{:S(2)}, u32[]{:S(2)}) %collective-permute-start.31) | collective-permute-done | bytes 262176 | tf_op jit(solution)/shard_map/ppermute | solution.py:54
  (56 shorter events, 29.6 us)
Async XLA Ops:
  1.3 11.1 %collective-permute-start.4 = (bf16[2,256,256]{2,1,0:T(8,128)(2,1)S(1)}, bf16[2,256,256]{2,1,0:T(8,128)(2,1)S(1)}, u32[]{:S(2)}, u32[]{:S(2)}) collective-permute-start(bf16[2,256,256]{2,1,0:T(8,128)(2,1)S(1)} %get-tuple-element.60), channel_id=1, source_target_pairs={{4,0},{8,4},{12,8},{16,12},{20,16},{24,20},{28,24},{32,28},{36,32}... | collective-permute-start | bytes 786440 | tf_op jit(solution)/shard_map/ppermute | solution.py:54
  8.5 10.1 %collective-permute-start = (bf16[2,256,256]{2,1,0:T(8,128)(2,1)S(1)}, bf16[2,256,256]{2,1,0:T(8,128)(2,1)S(1)}, u32[]{:S(2)}, u32[]{:S(2)}) collective-permute-start(bf16[2,256,256]{2,1,0:T(8,128)(2,1)S(1)} %get-tuple-element.53), channel_id=1, source_target_pairs={{4,0},{8,4},{12,8},{16,12},{20,16},{24,20},{28,24},{32,28},{36,32}... | collective-permute-start | bytes 786440 | tf_op jit(solution)/shard_map/ppermute | solution.py:54
  13.8 13.1 %collective-permute-start.5 = (bf16[2,256,256]{2,1,0:T(8,128)(2,1)S(1)}, bf16[2,256,256]{2,1,0:T(8,128)(2,1)S(1)}, u32[]{:S(2)}, u32[]{:S(2)}) collective-permute-start(bf16[2,256,256]{2,1,0:T(8,128)(2,1)S(1)} %get-tuple-element.62), channel_id=1, source_target_pairs={{0,1},{1,2},{2,3},{3,0},{4,5},{5,6},{6,7},{7,4},{8,9},{9,10},{10,1... | collective-permute-start | bytes 786440 | tf_op jit(solution)/shard_map/ppermute | solution.py:48
  15.3 13.4 %collective-permute-start.6 = (bf16[2,256,256]{2,1,0:T(8,128)(2,1)S(1)}, bf16[2,256,256]{2,1,0:T(8,128)(2,1)S(1)}, u32[]{:S(2)}, u32[]{:S(2)}) collective-permute-start(bf16[2,256,256]{2,1,0:T(8,128)(2,1)S(1)} %get-tuple-element.63), channel_id=1, source_target_pairs={{0,2},{1,3},{2,0},{3,1},{4,6},{5,7},{6,4},{7,5},{8,10},{9,11},{10,... | collective-permute-start | bytes 786440 | tf_op jit(solution)/shard_map/ppermute | solution.py:48
  16.4 15.6 %collective-permute-start.7 = (bf16[2,256,256]{2,1,0:T(8,128)(2,1)S(1)}, bf16[2,256,256]{2,1,0:T(8,128)(2,1)S(1)}, u32[]{:S(2)}, u32[]{:S(2)}) collective-permute-start(bf16[2,256,256]{2,1,0:T(8,128)(2,1)S(1)} %get-tuple-element.64), channel_id=1, source_target_pairs={{0,3},{1,0},{2,1},{3,2},{4,7},{5,4},{6,5},{7,6},{8,11},{9,8},{10,9... | collective-permute-start | bytes 786440 | tf_op jit(solution)/shard_map/ppermute | solution.py:48
  19.3 14.9 %collective-permute-start.1 = (bf16[2,256,256]{2,1,0:T(8,128)(2,1)S(1)}, bf16[2,256,256]{2,1,0:T(8,128)(2,1)S(1)}, u32[]{:S(2)}, u32[]{:S(2)}) collective-permute-start(bf16[2,256,256]{2,1,0:T(8,128)(2,1)S(1)} %get-tuple-element.57), channel_id=1, source_target_pairs={{0,1},{1,2},{2,3},{3,0},{4,5},{5,6},{6,7},{7,4},{8,9},{9,10},{10,1... | collective-permute-start | bytes 786440 | tf_op jit(solution)/shard_map/ppermute | solution.py:48
  19.4 17.8 %collective-permute-start.2 = (bf16[2,256,256]{2,1,0:T(8,128)(2,1)S(1)}, bf16[2,256,256]{2,1,0:T(8,128)(2,1)S(1)}, u32[]{:S(2)}, u32[]{:S(2)}) collective-permute-start(bf16[2,256,256]{2,1,0:T(8,128)(2,1)S(1)} %get-tuple-element.58), channel_id=1, source_target_pairs={{0,2},{1,3},{2,0},{3,1},{4,6},{5,7},{6,4},{7,5},{8,10},{9,11},{10,... | collective-permute-start | bytes 786440 | tf_op jit(solution)/shard_map/ppermute | solution.py:48
  26.9 12.6 %collective-permute-start.3 = (bf16[2,256,256]{2,1,0:T(8,128)(2,1)S(1)}, bf16[2,256,256]{2,1,0:T(8,128)(2,1)S(1)}, u32[]{:S(2)}, u32[]{:S(2)}) collective-permute-start(bf16[2,256,256]{2,1,0:T(8,128)(2,1)S(1)} %get-tuple-element.59), channel_id=1, source_target_pairs={{0,3},{1,0},{2,1},{3,2},{4,7},{5,4},{6,5},{7,6},{8,11},{9,8},{10,9... | collective-permute-start | bytes 786440 | tf_op jit(solution)/shard_map/ppermute | solution.py:48
  39.9 17.3 %collective-permute-start.8 = (bf16[2,256,256]{2,1,0:T(8,128)(2,1)S(1)}, bf16[2,256,256]{2,1,0:T(8,128)(2,1)S(1)}, u32[]{:S(2)}, u32[]{:S(2)}) collective-permute-start(bf16[2,256,256]{2,1,0:T(8,128)(2,1)S(1)} %get-tuple-element.66), channel_id=1, source_target_pairs={{0,1},{1,2},{2,3},{3,0},{4,5},{5,6},{6,7},{7,4},{8,9},{9,10},{10,1... | collective-permute-start | bytes 786440 | tf_op jit(solution)/shard_map/ppermute | solution.py:48
  41.2 25.0 %collective-permute-start.9 = (bf16[2,256,256]{2,1,0:T(8,128)(2,1)S(1)}, bf16[2,256,256]{2,1,0:T(8,128)(2,1)S(1)}, u32[]{:S(2)}, u32[]{:S(2)}) collective-permute-start(bf16[2,256,256]{2,1,0:T(8,128)(2,1)S(1)} %get-tuple-element.67), channel_id=1, source_target_pairs={{0,2},{1,3},{2,0},{3,1},{4,6},{5,7},{6,4},{7,5},{8,10},{9,11},{10,... | collective-permute-start | bytes 786440 | tf_op jit(solution)/shard_map/ppermute | solution.py:48
  52.1 14.1 %collective-permute-start.10 = (bf16[2,256,256]{2,1,0:T(8,128)(2,1)S(1)}, bf16[2,256,256]{2,1,0:T(8,128)(2,1)S(1)}, u32[]{:S(2)}, u32[]{:S(2)}) collective-permute-start(bf16[2,256,256]{2,1,0:T(8,128)(2,1)S(1)} %get-tuple-element.68), channel_id=1, source_target_pairs={{0,3},{1,0},{2,1},{3,2},{4,7},{5,4},{6,5},{7,6},{8,11},{9,8},{10,9... | collective-permute-start | bytes 786440 | tf_op jit(solution)/shard_map/ppermute | solution.py:48
  52.1 21.5 %collective-permute-start.13 = (bf16[2,256,256]{2,1,0:T(8,128)(2,1)S(1)}, bf16[2,256,256]{2,1,0:T(8,128)(2,1)S(1)}, u32[]{:S(2)}, u32[]{:S(2)}) collective-permute-start(bf16[2,256,256]{2,1,0:T(8,128)(2,1)S(1)} %get-tuple-element.73), channel_id=1, source_target_pairs={{0,1},{1,2},{2,3},{3,0},{4,5},{5,6},{6,7},{7,4},{8,9},{9,10},{10,1... | collective-permute-start | bytes 786440 | tf_op jit(solution)/shard_map/ppermute | solution.py:48
  54.1 19.5 %collective-permute-start.14 = (bf16[2,256,256]{2,1,0:T(8,128)(2,1)S(1)}, bf16[2,256,256]{2,1,0:T(8,128)(2,1)S(1)}, u32[]{:S(2)}, u32[]{:S(2)}) collective-permute-start(bf16[2,256,256]{2,1,0:T(8,128)(2,1)S(1)} %get-tuple-element.74), channel_id=1, source_target_pairs={{0,2},{1,3},{2,0},{3,1},{4,6},{5,7},{6,4},{7,5},{8,10},{9,11},{10,... | collective-permute-start | bytes 786440 | tf_op jit(solution)/shard_map/ppermute | solution.py:48
  57.2 17.7 %collective-permute-start.15 = (bf16[2,256,256]{2,1,0:T(8,128)(2,1)S(1)}, bf16[2,256,256]{2,1,0:T(8,128)(2,1)S(1)}, u32[]{:S(2)}, u32[]{:S(2)}) collective-permute-start(bf16[2,256,256]{2,1,0:T(8,128)(2,1)S(1)} %get-tuple-element.75), channel_id=1, source_target_pairs={{0,3},{1,0},{2,1},{3,2},{4,7},{5,4},{6,5},{7,6},{8,11},{9,8},{10,9... | collective-permute-start | bytes 786440 | tf_op jit(solution)/shard_map/ppermute | solution.py:48
  67.2 8.4 %collective-permute-start.12 = (bf16[2,256,256]{2,1,0:T(8,128)(2,1)S(1)}, bf16[2,256,256]{2,1,0:T(8,128)(2,1)S(1)}, u32[]{:S(2)}, u32[]{:S(2)}) collective-permute-start(bf16[2,256,256]{2,1,0:T(8,128)(2,1)S(1)} %get-tuple-element.71), channel_id=1, source_target_pairs={{4,0},{8,4},{12,8},{16,12},{20,16},{24,20},{28,24},{32,28},{36,32}... | collective-permute-start | bytes 786440 | tf_op jit(solution)/shard_map/ppermute | solution.py:54
  71.7 9.8 %collective-permute-start.11 = (bf16[2,256,256]{2,1,0:T(8,128)(2,1)S(1)}, bf16[2,256,256]{2,1,0:T(8,128)(2,1)S(1)}, u32[]{:S(2)}, u32[]{:S(2)}) collective-permute-start(bf16[2,256,256]{2,1,0:T(8,128)(2,1)S(1)} %get-tuple-element.70.rest_3_), channel_id=1, source_target_pairs={{0,4},{4,8},{8,12},{12,16},{16,20},{20,24},{24,28},{28,32},{32,36}... | collective-permute-start | bytes 786440 | tf_op jit(solution)/shard_map/ppermute | solution.py:54
  82.8 8.3 %collective-permute-start.20 = (bf16[2,256,256]{2,1,0:T(8,128)(2,1)S(1)}, bf16[2,256,256]{2,1,0:T(8,128)(2,1)S(1)}, u32[]{:S(2)}, u32[]{:S(2)}) collective-permute-start(bf16[2,256,256]{2,1,0:T(8,128)(2,1)S(1)} %get-tuple-element.83), channel_id=1, source_target_pairs={{4,0},{8,4},{12,8},{16,12},{20,16},{24,20},{28,24},{32,28},{36,32}... | collective-permute-start | bytes 786440 | tf_op jit(solution)/shard_map/ppermute | solution.py:54
  84.7 9.8 %collective-permute-start.19 = (bf16[2,256,256]{2,1,0:T(8,128)(2,1)S(1)}, bf16[2,256,256]{2,1,0:T(8,128)(2,1)S(1)}, u32[]{:S(2)}, u32[]{:S(2)}) collective-permute-start(bf16[2,256,256]{2,1,0:T(8,128)(2,1)S(1)} %get-tuple-element.82.spill_ref), channel_id=1, source_target_pairs={{0,4},{4,8},{8,12},{12,16},{16,20},{20,24},{24,28},{28,32},{32,36}... | collective-permute-start | bytes 786440 | tf_op jit(solution)/shard_map/ppermute | solution.py:54
  87.1 10.2 %collective-permute-start.16 = (bf16[2,256,256]{2,1,0:T(8,128)(2,1)S(1)}, bf16[2,256,256]{2,1,0:T(8,128)(2,1)S(1)}, u32[]{:S(2)}, u32[]{:S(2)}) collective-permute-start(bf16[2,256,256]{2,1,0:T(8,128)(2,1)S(1)} %get-tuple-element.78), channel_id=1, source_target_pairs={{0,1},{1,2},{2,3},{3,0},{4,5},{5,6},{6,7},{7,4},{8,9},{9,10},{10,1... | collective-permute-start | bytes 786440 | tf_op jit(solution)/shard_map/ppermute | solution.py:48
  87.2 12.1 %collective-permute-start.17 = (bf16[2,256,256]{2,1,0:T(8,128)(2,1)S(1)}, bf16[2,256,256]{2,1,0:T(8,128)(2,1)S(1)}, u32[]{:S(2)}, u32[]{:S(2)}) collective-permute-start(bf16[2,256,256]{2,1,0:T(8,128)(2,1)S(1)} %get-tuple-element.79), channel_id=1, source_target_pairs={{0,2},{1,3},{2,0},{3,1},{4,6},{5,7},{6,4},{7,5},{8,10},{9,11},{10,... | collective-permute-start | bytes 786440 | tf_op jit(solution)/shard_map/ppermute | solution.py:48
  89.1 14.6 %collective-permute-start.18 = (bf16[2,256,256]{2,1,0:T(8,128)(2,1)S(1)}, bf16[2,256,256]{2,1,0:T(8,128)(2,1)S(1)}, u32[]{:S(2)}, u32[]{:S(2)}) collective-permute-start(bf16[2,256,256]{2,1,0:T(8,128)(2,1)S(1)} %get-tuple-element.80), channel_id=1, source_target_pairs={{0,3},{1,0},{2,1},{3,2},{4,7},{5,4},{6,5},{7,6},{8,11},{9,8},{10,9... | collective-permute-start | bytes 786440 | tf_op jit(solution)/shard_map/ppermute | solution.py:48
  95.4 12.3 %collective-permute-start.21 = (bf16[2,256,256]{2,1,0:T(8,128)(2,1)S(1)}, bf16[2,256,256]{2,1,0:T(8,128)(2,1)S(1)}, u32[]{:S(2)}, u32[]{:S(2)}) collective-permute-start(bf16[2,256,256]{2,1,0:T(8,128)(2,1)S(1)} %get-tuple-element.85), channel_id=1, source_target_pairs={{0,1},{1,2},{2,3},{3,0},{4,5},{5,6},{6,7},{7,4},{8,9},{9,10},{10,1... | collective-permute-start | bytes 786440 | tf_op jit(solution)/shard_map/ppermute | solution.py:48
  95.5 13.8 %collective-permute-start.22 = (bf16[2,256,256]{2,1,0:T(8,128)(2,1)S(1)}, bf16[2,256,256]{2,1,0:T(8,128)(2,1)S(1)}, u32[]{:S(2)}, u32[]{:S(2)}) collective-permute-start(bf16[2,256,256]{2,1,0:T(8,128)(2,1)S(1)} %get-tuple-element.86), channel_id=1, source_target_pairs={{0,2},{1,3},{2,0},{3,1},{4,6},{5,7},{6,4},{7,5},{8,10},{9,11},{10,... | collective-permute-start | bytes 786440 | tf_op jit(solution)/shard_map/ppermute | solution.py:48
  97.4 16.3 %collective-permute-start.23 = (bf16[2,256,256]{2,1,0:T(8,128)(2,1)S(1)}, bf16[2,256,256]{2,1,0:T(8,128)(2,1)S(1)}, u32[]{:S(2)}, u32[]{:S(2)}) collective-permute-start(bf16[2,256,256]{2,1,0:T(8,128)(2,1)S(1)} %get-tuple-element.87), channel_id=1, source_target_pairs={{0,3},{1,0},{2,1},{3,2},{4,7},{5,4},{6,5},{7,6},{8,11},{9,8},{10,9... | collective-permute-start | bytes 786440 | tf_op jit(solution)/shard_map/ppermute | solution.py:48
  114.0 16.9 %collective-permute-start.24 = (bf16[2,256,256]{2,1,0:T(8,128)(2,1)S(1)}, bf16[2,256,256]{2,1,0:T(8,128)(2,1)S(1)}, u32[]{:S(2)}, u32[]{:S(2)}) collective-permute-start(bf16[2,256,256]{2,1,0:T(8,128)(2,1)S(1)} %get-tuple-element.89), channel_id=1, source_target_pairs={{0,1},{1,2},{2,3},{3,0},{4,5},{5,6},{6,7},{7,4},{8,9},{9,10},{10,1... | collective-permute-start | bytes 786440 | tf_op jit(solution)/shard_map/ppermute | solution.py:48
  115.0 25.0 %collective-permute-start.25 = (bf16[2,256,256]{2,1,0:T(8,128)(2,1)S(1)}, bf16[2,256,256]{2,1,0:T(8,128)(2,1)S(1)}, u32[]{:S(2)}, u32[]{:S(2)}) collective-permute-start(bf16[2,256,256]{2,1,0:T(8,128)(2,1)S(1)} %get-tuple-element.90), channel_id=1, source_target_pairs={{0,2},{1,3},{2,0},{3,1},{4,6},{5,7},{6,4},{7,5},{8,10},{9,11},{10,... | collective-permute-start | bytes 786440 | tf_op jit(solution)/shard_map/ppermute | solution.py:48
  126.0 13.9 %collective-permute-start.26 = (bf16[2,256,256]{2,1,0:T(8,128)(2,1)S(1)}, bf16[2,256,256]{2,1,0:T(8,128)(2,1)S(1)}, u32[]{:S(2)}, u32[]{:S(2)}) collective-permute-start(bf16[2,256,256]{2,1,0:T(8,128)(2,1)S(1)} %get-tuple-element.91), channel_id=1, source_target_pairs={{0,3},{1,0},{2,1},{3,2},{4,7},{5,4},{6,5},{7,6},{8,11},{9,8},{10,9... | collective-permute-start | bytes 786440 | tf_op jit(solution)/shard_map/ppermute | solution.py:48
  126.0 17.4 %collective-permute-start.28 = (bf16[2,256,256]{2,1,0:T(8,128)(2,1)S(1)}, bf16[2,256,256]{2,1,0:T(8,128)(2,1)S(1)}, u32[]{:S(2)}, u32[]{:S(2)}) collective-permute-start(bf16[2,256,256]{2,1,0:T(8,128)(2,1)S(1)} %get-tuple-element.96), channel_id=1, source_target_pairs={{0,1},{1,2},{2,3},{3,0},{4,5},{5,6},{6,7},{7,4},{8,9},{9,10},{10,1... | collective-permute-start | bytes 786440 | tf_op jit(solution)/shard_map/ppermute | solution.py:48
  128.1 16.5 %collective-permute-start.29 = (bf16[2,256,256]{2,1,0:T(8,128)(2,1)S(1)}, bf16[2,256,256]{2,1,0:T(8,128)(2,1)S(1)}, u32[]{:S(2)}, u32[]{:S(2)}) collective-permute-start(bf16[2,256,256]{2,1,0:T(8,128)(2,1)S(1)} %get-tuple-element.97), channel_id=1, source_target_pairs={{0,2},{1,3},{2,0},{3,1},{4,6},{5,7},{6,4},{7,5},{8,10},{9,11},{10,... | collective-permute-start | bytes 786440 | tf_op jit(solution)/shard_map/ppermute | solution.py:48
  130.9 18.8 %collective-permute-start.30 = (bf16[2,256,256]{2,1,0:T(8,128)(2,1)S(1)}, bf16[2,256,256]{2,1,0:T(8,128)(2,1)S(1)}, u32[]{:S(2)}, u32[]{:S(2)}) collective-permute-start(bf16[2,256,256]{2,1,0:T(8,128)(2,1)S(1)} %get-tuple-element.98), channel_id=1, source_target_pairs={{0,3},{1,0},{2,1},{3,2},{4,7},{5,4},{6,5},{7,6},{8,11},{9,8},{10,9... | collective-permute-start | bytes 786440 | tf_op jit(solution)/shard_map/ppermute | solution.py:48
  141.5 11.6 %collective-permute-start.27 = (bf16[2,256,256]{2,1,0:T(8,128)(2,1)S(1)}, bf16[2,256,256]{2,1,0:T(8,128)(2,1)S(1)}, u32[]{:S(2)}, u32[]{:S(2)}) collective-permute-start(bf16[2,256,256]{2,1,0:T(8,128)(2,1)S(1)} %get-tuple-element.93), channel_id=1, source_target_pairs={{0,4},{4,8},{8,12},{12,16},{16,20},{20,24},{24,28},{28,32},{32,36}... | collective-permute-start | bytes 786440 | tf_op jit(solution)/shard_map/ppermute | solution.py:54
  151.3 9.8 %collective-permute-start.31 = (bf16[2,256,256]{2,1,0:T(8,128)(2,1)S(1)}, bf16[2,256,256]{2,1,0:T(8,128)(2,1)S(1)}, u32[]{:S(2)}, u32[]{:S(2)}) collective-permute-start(bf16[2,256,256]{2,1,0:T(8,128)(2,1)S(1)} %get-tuple-element.100), channel_id=1, source_target_pairs={{0,4},{4,8},{8,12},{12,16},{16,20},{20,24},{24,28},{28,32},{32,36}... | collective-permute-start | bytes 786440 | tf_op jit(solution)/shard_map/ppermute | solution.py:54
  (6 other events, 122.9 us)
